TPU v7x, 512 devices: a whole 4x4x16 slice. The times are simulated.
512 devices in a mesh: ind: 16 (over y, x), blk: 32 (over z, core).
Axes of the slice: x: 4, y: 4, z: 16, core: 2. Of those that a mesh axis runs over, the one named last changes fastest.
Arguments:
- dosage: bfloat16 [8192, 32768], P('ind', 'blk'), may hold values from 0 to 2
- residual: float32 [8192], P('ind'), may hold values from -9 to 9
- pairs: int32 [512, 2], P('blk'), may hold values from 0 to 127, as said below
- counts: int32 [32], P('blk'), may hold values from 12 to 16, as said below
Outputs:
- scores: bfloat16 [256, 512, 256], P('ind', 'blk')
Inputs may be any that keep to these rules, and one draw needn't show every extreme that they name: For slot p, pairs[p, 0] is one of the blocks p div 16 * 4 to p div 16 * 4 + 3; the live slots of one owner have second blocks pairs[p, 1] with distinct values of pairs[p, 1] div 4. `counts`: some owner has exactly 16 live slots.
All inputs are finite; a program needn't handle non-finite values.
Results may differ from a plain program's by a relative error of at most 0.018.
Values may be sent and summed in bfloat16 or wider, within the bound.
No kernel may reach another device: no remote copies, remote signals or barrier semaphores. Data moves between devices by JAX's collectives and lax.ppermute only.
A program may use at most 64 MiB of HBM per device.

v0:
```python
import jax
import jax.numpy as jnp
from jax import lax
from jax.sharding import Mesh
from jax.sharding import PartitionSpec as P

B = 256
BLK = ("blk_0", "blk_1")


EPSILON = 1e-05


def cut_along(shard, dim, size):
    dims = shard.shape
    parts = shard.reshape(*dims[:dim], size, dims[dim] // size, *dims[dim + 1 :])
    return jnp.moveaxis(parts, dim, 0)


def joined_along(parts, dim):
    dims = list(parts.shape[1:])
    dims[dim] *= parts.shape[0]
    return jnp.moveaxis(parts, 0, dim).reshape(dims)


def exchange_in_order(parts, axes, turns):
    dims = [lax.axis_size(a) for a in axes]
    parts = parts.reshape(*dims, *parts.shape[1:])
    for k in turns:
        parts = lax.all_to_all(parts, axes[k], split_axis=k, concat_axis=k, tiled=True)
    return parts.reshape(-1, *parts.shape[len(axes) :])


def exchange_by_chip(shard, groups, turns, split_dim, concat_dim):
    size = lax.axis_size(groups[0]) * lax.axis_size(groups[1])
    parts = cut_along(shard, split_dim, size)
    return joined_along(exchange_in_order(parts, groups, turns), concat_dim)


def summed_on_arrival(shard, axis, dim):
    size = lax.axis_size(axis)
    parts = lax.all_to_all(cut_along(shard, dim, size), axis, 0, 0, tiled=True)
    return jnp.sum(parts.astype(jnp.float32), axis=0)


def tile_terms(left, left_sq, right, right_sq):
    cross = jnp.einsum("nsa,nsc->asc", left, right, preferred_element_type=jnp.float32)
    spread = jnp.einsum("nsa,nsc->asc", left_sq, right_sq, preferred_element_type=jnp.float32)
    return jnp.stack([cross, spread], axis=1)


def squared(values):
    return (values.astype(jnp.float32) ** 2).astype(jnp.bfloat16)


def on_device(dosage, residual, pairs, counts):
    group_count = lax.axis_size(BLK)
    member = lax.axis_index(BLK)
    row_count, width = dosage.shape
    block_width = B
    local_blocks = width // block_width
    slot_count = pairs.shape[0]
    blocks = dosage.reshape(row_count, local_blocks, block_width)
    live = jnp.arange(slot_count, dtype=jnp.int32) < counts[0]
    first_local = pairs[:, 0] - member * local_blocks
    left_raw = jnp.take(blocks, first_local, axis=1)
    left = (residual[:, None, None] * left_raw.astype(jnp.float32)).astype(jnp.bfloat16)
    left_sq = squared(left)
    holder = pairs[:, 1] // local_blocks
    second_local = pairs[:, 1] % local_blocks
    match = (holder[None, :] == jnp.arange(group_count, dtype=jnp.int32)[:, None]) & live[None, :]
    request = jnp.sum(jnp.where(match, second_local[None, :] + 1, 0), axis=1) - 1
    wanted = exchange_by_chip(request, ("blk_0", "blk_1"), (1, 0), 0, 0)
    outgoing = jnp.take(blocks, jnp.maximum(wanted, 0), axis=1)
    incoming = lax.all_to_all(outgoing, BLK, split_axis=1, concat_axis=1, tiled=True)
    right = jnp.take(incoming, holder, axis=1)
    right_sq = squared(right)
    summed = summed_on_arrival(
        tile_terms(left, left_sq, right, right_sq).astype(jnp.bfloat16), "ind", 0
    )
    cross = summed[:, 0]
    spread = summed[:, 1]
    total_rows = row_count * lax.axis_size("ind")
    ratio = cross / jnp.sqrt(spread + EPSILON * total_rows)
    return jnp.where(live[None, :, None], ratio, jnp.float32(0.0)).astype(jnp.bfloat16)


def solution(mesh):
    torus = Mesh(mesh.devices.reshape(mesh.shape["ind"], 16, 2), ("ind", "blk_0", "blk_1"))
    placed = (P("ind", BLK), P("ind"), P(BLK, None), P(BLK))
    return jax.shard_map(
        on_device, mesh=torus, in_specs=placed, out_specs=P("ind", BLK, None), check_vma=False
    )
```

profile of v0, /device:TPU:1, one launch (start us, length us, event | category | flops | bytes accessed | tf_op | source)
XLA Modules:
  0.0 486.9 jit_solution(111309426845995708)
XLA Ops:
  0.0 0.7 and_select_fusion.1
  1.4 0.1 select_reduce_fusion
  1.6 10.2 %all_to_all.20 = s32[16,2,1]{0,2,1:T(1,128)S(1)} all-to-all(s32[16,2,1]{0,2,1:T(1,128)S(1)} %copy.25), channel_id=1, replica_groups=mesh['ind'=16,'blk_0'=16,'blk_1'=2] {'blk_1'}, dimensions={1} | all-to-all | bytes 256 | tf_op jit(solution)/shard_map/all_to_all | solution.py:30
  11.8 0.7 copy.26
  12.5 9.6 %all-to-all-start.1 = ((s32[16,2,1]{1,2,0:T(1,128)}), s32[16,2,1]{1,2,0:T(1,128)S(1)}, u32[]{:S(2)}, u32[]{:S(2)}) async-start(s32[16,2,1]{1,2,0:T(1,128)} %copy.26), calls=%async_computation.1 | async-start | bytes 16384 | tf_op jit(solution)/shard_map/all_to_all | solution.py:30
  22.1 1.5 copy.27
  23.6 0.5 copy.28
  24.1 9.2 %all-to-all-done.1 = s32[16,2,1]{1,2,0:T(1,128)S(1)} async-done(((s32[16,2,1]{1,2,0:T(1,128)}), s32[16,2,1]{1,2,0:T(1,128)S(1)}, u32[]{:S(2)}, u32[]{:S(2)}) %all-to-all-start.1) | async-done | bytes 160 | tf_op jit(solution)/shard_map/all_to_all | solution.py:30
  33.5 0.1 le.29
  33.6 4.9 gather_fusion
  38.5 7.5 %select_bitcast_fusion = bf16[512,32,256]{2,0,1:T(8,128)(2,1)} fusion(bf16[32,512,256]{2,1,0:T(8,128)(2,1)} %gather_fusion, pred[32]{0:T(512)(128)(4,1)S(1)} %le.29), kind=kLoop, calls=%fused_computation.4 | loop fusion | flops 4194304 | bytes 16777248 | tf_op jit(solution)/shard_map/jit(_take)/select_n | solution.py:74
  45.9 6.4 %all-to-all-start.2 = ((bf16[512,32,256]{2,0,1:T(8,128)(2,1)}), bf16[512,32,256]{2,0,1:T(8,128)(2,1)}, u32[]{:S(2)}, u32[]{:S(2)}) async-start(bf16[512,32,256]{2,0,1:T(8,128)(2,1)} %select_bitcast_fusion), calls=%async_computation.2 | async-start | bytes 16777216 | tf_op jit(solution)/shard_map/all_to_all | solution.py:75
  52.4 2.7 gather_fusion.2
  55.1 357.7 %all-to-all-done.2 = bf16[512,32,256]{2,0,1:T(8,128)(2,1)} async-done(((bf16[512,32,256]{2,0,1:T(8,128)(2,1)}), bf16[512,32,256]{2,0,1:T(8,128)(2,1)}, u32[]{:S(2)}, u32[]{:S(2)}) %all-to-all-start.2) | async-done | bytes 8388640 | tf_op jit(solution)/shard_map/all_to_all | solution.py:75
  412.8 6.2 %gather_fusion.1 = bf16[16,512,256]{2,1,0:T(8,128)(2,1)} fusion(bf16[512,32,256]{2,0,1:T(8,128)(2,1)} %all-to-all-done.2, s32[1024]{0:T(1024)S(1)} %pad_clamp_fusion.1), kind=kCustom, calls=%fused_computation.1 | custom fusion | bytes 8388672 | tf_op jit(solution)/shard_map/jit(_take)/gather | solution.py:76
  419.0 5.7 %fusion.5 = bf16[16,256,256]{1,2,0:T(8,128)(2,1)S(1)} fusion(bf16[16,512,256]{2,1,0:T(8,128)(2,1)} %gather_fusion.1, pred[16]{0:T(512)(128)(4,1)S(1)} %get-tuple-element.11, f32[512]{0:T(512)S(1)} %copy-done.3, bf16[16,512,256]{2,1,0:T(8,128)(2,1)} %gather_fusion.2, pred[16]{0:T(512)(128)(4,1)S(1)} %get-tuple-element.5), kind=kOutput, calls=%fused_computation.15 | convolution fusion | flops 1085276160 | bytes 10487840 | tf_op jit(solution)/shard_map/nsa,nsc->asc/dot_general | solution.py:47
  424.7 0.2 copy-done.1
  424.9 3.2 fusion.8
  428.1 0.4 pad_maximum_fusion
  428.5 0.5 copy.38
  429.1 56.5 %all_to_all.21 = bf16[16,16,2,16,256]{4,1,3,2,0:T(8,128)(2,1)S(1)} all-to-all(bf16[16,16,2,16,256]{4,1,3,2,0:T(8,128)(2,1)S(1)} %copy.38), channel_id=1, replica_groups=mesh['ind'=16,'blk_0'=16,'blk_1'=2] {'ind'}, dimensions={0} | all-to-all | bytes 8388608 | tf_op jit(solution)/shard_map/all_to_all | solution.py:42
  485.6 0.6 convert_reduce_fusion
  486.2 0.1 fusion.13
  486.2 0.7 copy.35
  (19 shorter events, 0.4 us)
Async XLA Ops:
  12.5 20.8 %all-to-all-start.1 = ((s32[16,2,1]{1,2,0:T(1,128)}), s32[16,2,1]{1,2,0:T(1,128)S(1)}, u32[]{:S(2)}, u32[]{:S(2)}) async-start(s32[16,2,1]{1,2,0:T(1,128)} %copy.26), calls=%async_computation.1 | async-start | bytes 16384 | tf_op jit(solution)/shard_map/all_to_all | solution.py:30
  45.9 6.4 %copy-start.2 = (s32[16,2]{0,1:T(2,128)S(1)}, s32[16,2]{0,1:T(2,128)}, u32[]{:S(2)}) copy-start(s32[16,2]{0,1:T(2,128)} %param.6) | copy-start | bytes 388
  45.9 366.9 %all-to-all-start.2 = ((bf16[512,32,256]{2,0,1:T(8,128)(2,1)}), bf16[512,32,256]{2,0,1:T(8,128)(2,1)}, u32[]{:S(2)}, u32[]{:S(2)}) async-start(bf16[512,32,256]{2,0,1:T(8,128)(2,1)} %select_bitcast_fusion), calls=%async_computation.2 | async-start | bytes 16777216 | tf_op jit(solution)/shard_map/all_to_all | solution.py:75
  55.1 363.9 %copy-start.3 = (f32[512]{0:T(512)S(1)}, f32[512]{0:T(512)}, u32[]{:S(2)}) copy-start(f32[512]{0:T(512)} %param.5) | copy-start | bytes 6148
  419.0 5.7 %copy-start = (bf16[16,512,256]{2,1,0:T(8,128)(2,1)S(1)}, bf16[16,512,256]{2,1,0:T(8,128)(2,1)}, u32[]{:S(2)}) copy-start(bf16[16,512,256]{2,1,0:T(8,128)(2,1)} %gather_fusion.2) | copy-start | bytes 12582916
  419.0 5.9 %copy-start.1 = (bf16[16,512,256]{2,1,0:T(8,128)(2,1)S(1)}, bf16[16,512,256]{2,1,0:T(8,128)(2,1)}, u32[]{:S(2)}) copy-start(bf16[16,512,256]{2,1,0:T(8,128)(2,1)} %gather_fusion.1) | copy-start | bytes 12582916
where the time goes:
time: 496 us; the launch traced here: 487 us
  waiting for transfers between devices  367 us (74%)
  blocking collectives  66.7 us (13%)
  local copies, waits for them, and re-layouts  18.3 us (4%)
  starting transfers between devices  16 us (3%)
  other arithmetic  9.42 us (2%)
  matrix products  8.86 us (2%)
    all_to_all x1, waiting for transfers between devices, on_device(): lax.all_to_all(outgoing, BLK, split_axis=1, concat_axis=1, tiled=True)  358 us
    all_to_all x1, blocking collectives, summed_on_arrival(): parts = lax.all_to_all(cut_along(shard, dim, size), axis, 0, 0, tiled=True)  56.5 us
    all_to_all x1, blocking collectives, exchange_in_order(): lax.all_to_all(parts, axes[k], split_axis=k, concat_axis=k, tiled=True)  10.2 us
  transfers between devices with their start and end apart: 2, of which 2 were waited for; matrix products, arithmetic and copies ran while one was open for 1% of the time, Pallas kernels for 0%

commit v1 on v0

v1 whole, which is shorter than its diff:
```python
import functools

import jax
import jax.numpy as jnp
from jax import lax
from jax.experimental import pallas as pl
from jax.experimental.pallas import tpu as pltpu
from jax.sharding import Mesh
from jax.sharding import PartitionSpec as P

B = 256
EPSILON = 1e-05


def tile_kernel(cells, ring, table, place, residual, *refs):
    count = len(cells)
    out = refs[2 * count]
    parts = out.shape[0]
    for j in range(count):
        a_ref, c_ref = refs[2 * j], refs[2 * j + 1]
        entry = table[entry_at(cells[j], ring, place)]

        @pl.when(entry > 0)
        def _(a_ref=a_ref, c_ref=c_ref, j=j):
            weighted = (residual[...] * a_ref[...].astype(jnp.float32)).astype(jnp.bfloat16)
            right = c_ref[...]
            over_rows = (((0,), (0,)), ((), ()))
            cross = lax.dot_general(
                weighted, right, over_rows, preferred_element_type=jnp.float32
            )
            spread = lax.dot_general(
                weighted * weighted, right * right, over_rows, preferred_element_type=jnp.float32
            )
            out[:, j, 0] = cross.astype(jnp.bfloat16).reshape(parts, B // parts, B)
            out[:, j, 1] = spread.astype(jnp.bfloat16).reshape(parts, B // parts, B)

        @pl.when(entry == 0)
        def _(j=j):
            out[:, j] = jnp.zeros((parts, 2, B // parts, B), jnp.bfloat16)


def entry_at(cell, ring, place):
    distance, to_owner, other = cell
    owner = lax.rem(place[0] + (to_owner % ring), ring)
    core = place[1] if not other else 1 - place[1]
    return (owner * ring + (distance % ring)) * 2 + core


def tiles(cells, ring, parts, table, place, residual, operands):
    rows = residual.shape[0]

    def first_map(cell, i, table, place):
        entry = table[entry_at(cell, ring, place)]
        return (0, jnp.maximum(entry - 1, 0) // 4)

    def second_map(cell, i, table, place):
        entry = table[entry_at(cell, ring, place)]
        return (0, lax.rem(jnp.maximum(entry - 1, 0), 4))

    specs, arrays = [], []
    for cell, (a, c) in zip(cells, operands):
        specs.append(pl.BlockSpec((rows, B), functools.partial(first_map, cell)))
        specs.append(pl.BlockSpec((rows, B), functools.partial(second_map, cell)))
        arrays += [a, c]
    shape = (parts, len(cells), 2, B // parts, B)
    return pl.pallas_call(
        functools.partial(tile_kernel, cells, ring),
        out_shape=jax.ShapeDtypeStruct(shape, jnp.bfloat16),
        grid_spec=pltpu.PrefetchScalarGridSpec(
            num_scalar_prefetch=2,
            grid=(1,),
            in_specs=[pl.BlockSpec((rows, 1), lambda i, t, p: (0, 0))] + specs,
            out_specs=pl.BlockSpec(shape, lambda i, t, p: (0, 0, 0, 0, 0)),
        ),
        cost_estimate=pl.CostEstimate(
            flops=len(cells) * 4 * rows * B * B,
            bytes_accessed=len(cells) * (2 * rows * B * 2 + 2 * B * B * 2),
            transcendentals=0,
        ),
        compiler_params=pltpu.CompilerParams(vmem_limit_bytes=60 << 20),
    )(table, place, residual, *arrays)


def on_device(dosage, residual, pairs, counts):
    ring = lax.axis_size("z")
    parts = lax.axis_size("ind")
    chip, core = lax.axis_index("z"), lax.axis_index("core")
    total_rows = dosage.shape[0] * parts
    local_blocks = dosage.shape[1] // B
    slot_count = pairs.shape[0]

    live = jnp.arange(slot_count, dtype=jnp.int32) < counts[0]
    first_local = pairs[:, 0] - (chip * 2 + core) * local_blocks
    second_local = pairs[:, 1] % local_blocks
    holder = pairs[:, 1] // local_blocks
    away = (holder // 2 - chip) % ring
    position = away * 2 + holder % 2
    wanted = (position[:, None] == jnp.arange(2 * ring, dtype=jnp.int32)[None, :]) & live[:, None]
    code = 1 + first_local * local_blocks + second_local
    row = jnp.sum(jnp.where(wanted, code[:, None], 0), axis=0)
    table = lax.all_gather(row, "z", axis=0, tiled=True)
    place = jnp.stack([chip, core]).astype(jnp.int32)
    column = residual[:, None]

    def shift(x, by):
        return lax.ppermute(x, "z", [(s, (s + by) % ring) for s in range(ring)])

    def swap(x):
        return lax.ppermute(x, "core", [(0, 1), (1, 0)])

    hops = ring // 4
    below, above = [dosage], [dosage]
    here = swap(dosage)
    below_other, above_other = [here], [here]
    results = {}
    for h in range(1, hops + 1):
        below.append(shift(below[h - 1], 1))
        above.append(shift(above[h - 1], -1))
        last = h == hops
        if not last:
            below_other.append(swap(below[h]))
        above_other.append(swap(above[h]))
        cells, operands = [], []

        def add(distance, to_owner, a, c, c_other):
            cells.append((distance, to_owner, False))
            operands.append((a, c))
            cells.append((distance, to_owner, True))
            operands.append((a, c_other))

        if h == 1:
            add(0, 0, dosage, dosage, here)
        add(2 * h - 1, -h, below[h], above[h - 1], above_other[h - 1])
        add(2 * h, -h, below[h], above[h], above_other[h])
        add(1 - 2 * h, h, above[h], below[h - 1], below_other[h - 1])
        if not last:
            add(-2 * h, h, above[h], below[h], below_other[h])
        partial = tiles(tuple(cells), ring, parts, table, place, column, operands)
        summed = lax.psum_scatter(partial, "ind", scatter_dimension=0, tiled=True)[0]
        summed = summed.astype(jnp.float32)
        scores = summed[:, 0] / jnp.sqrt(summed[:, 1] + EPSILON * total_rows)
        scores = scores.astype(jnp.bfloat16)
        at = 0
        if h == 1:
            results[0] = scores[0:2]
            at = 2
        back = shift(scores[at : at + 4], -h)
        results[2 * h - 1], results[2 * h] = back[0:2], back[2:4]
        at += 4
        back = shift(scores[at:], h)
        results[1 - 2 * h] = back[0:2]
        if not last:
            results[-2 * h] = back[2:4]
    found = jnp.concatenate([results[d if d <= 2 * hops else d - ring] for d in range(ring)], axis=0)
    index = away * 2 + jnp.where(holder % 2 == core, 0, 1)
    picked = jnp.take(found, index, axis=0)
    picked = jnp.where(live[:, None, None], picked, jnp.bfloat16(0.0))
    return jnp.transpose(picked, (1, 0, 2))


def solution(mesh):
    devices = mesh.devices.reshape(mesh.shape["ind"], mesh.shape["blk"] // 2, 2)
    torus = Mesh(devices, ("ind", "z", "core"))
    owners = ("z", "core")
    placed = (P("ind", owners), P("ind"), P(owners, None), P(owners))
    return jax.shard_map(
        on_device, mesh=torus, in_specs=placed, out_specs=P("ind", owners, None), check_vma=False
    )
```

time: 496 us -> 482 us (0.972); the launches traced: 487 us -> 478 us
  starting transfers between devices: 16 us -> 97.4 us
  waiting for transfers between devices: 367 us -> 299 us
  blocking collectives: 66.7 us -> 15 us
  Pallas kernels: 0 us -> 24.2 us
  between operations: 0.79 us -> 15.1 us
  matrix products: 8.86 us -> 0 us
    all_to_all x2 -> x0, waiting for transfers between devices: 367 us -> none  [the longest x1 358 us: on_device(): lax.all_to_all(outgoing, BLK, split_axis=1, concat_axis=1, tiled=True)]
    unnamed x0 -> x8, waiting for transfers between devices: none -> 210 us
    ppermute x0 -> x24, starting transfers between devices: none -> 97.3 us  [the longest x16 67.3 us: shift(): return lax.ppermute(x, 'z', [(s, (s + by) % ring) for s in range(ring)])]
    ppermute x0 -> x24, waiting for transfers between devices: none -> 88.6 us  [the longest x16 84 us: shift(): return lax.ppermute(x, 'z', [(s, (s + by) % ring) for s in range(ring)])]
    all_to_all x2 -> x0, blocking collectives: 66.7 us -> none  [the longest x1 56.5 us: summed_on_arrival(): parts = lax.all_to_all(cut_along(shard, dim, size), axis, 0, 0, tiled=True)]
    pallas_call x0 -> x4, Pallas kernels: none -> 24.2 us  [tiles(): pl.pallas_call(functools.partial(tile_kernel, cells, ring), out_shape=jax...]
    all_to_all x2 -> x0, starting transfers between devices: 16 us -> none  [the longest x1 9.57 us: exchange_in_order(): lax.all_to_all(parts, axes[k], split_axis=k, concat_axis=k, tiled=True)]
    unnamed x0 -> x1, blocking collectives: none -> 15 us
  transfers between devices with their start and end apart: 2 -> 28, of which waited for: 2 -> 15; matrix products, arithmetic and copies ran while one was open for 1% -> 3% of each run, Pallas kernels for 0% -> 4%
where the time goes in v1:
time: 482 us; the launch traced here: 478 us
  waiting for transfers between devices  299 us (62%)
  starting transfers between devices  97.4 us (20%)
  Pallas kernels  24.2 us (5%)
  local copies, waits for them, and re-layouts  22.7 us (5%)
  between operations  15.1 us (3%)
  blocking collectives  15 us (3%)
  other arithmetic  5.41 us (1%)
    unnamed x8, waiting for transfers between devices  210 us
    ppermute x16, waiting for transfers between devices, shift(): return lax.ppermute(x, 'z', [(s, (s + by) % ring) for s in range(ring)])  84 us
    ppermute x16, starting transfers between devices, shift(): return lax.ppermute(x, 'z', [(s, (s + by) % ring) for s in range(ring)])  67.3 us
    ppermute x8, starting transfers between devices, swap(): return lax.ppermute(x, 'core', [(0, 1), (1, 0)])  30 us
    pallas_call x4, Pallas kernels, tiles(): pl.pallas_call(functools.partial(tile_kernel, cells, ring), out_shape=jax...  24.2 us
    unnamed x1, blocking collectives  15 us
    pallas_call x3, local copies, waits for them, and re-layouts, tiles(): pl.pallas_call(functools.partial(tile_kernel, cells, ring), out_shape=jax...  10 us
    unnamed x54, local copies, waits for them, and re-layouts  9.86 us
  transfers between devices with their start and end apart: 28, of which 15 were waited for; matrix products, arithmetic and copies ran while one was open for 3% of the time, Pallas kernels for 4%

profile of v1, /device:TPU:1, one launch (start us, length us, event | category | flops | bytes accessed | tf_op | source)
XLA Modules:
  0.0 478.4 jit_solution(2074466564123600991)
XLA Ops:
  6.5 11.9 %collective-permute-start.2 = (bf16[512,1024]{1,0:T(8,128)(2,1)}, bf16[512,1024]{1,0:T(8,128)(2,1)S(1)}, u32[]{:S(2)}, u32[]{:S(2)}) collective-permute-start(bf16[512,1024]{1,0:T(8,128)(2,1)} %refs_13_.1), channel_id=1, source_target_pairs={{0,30},{2,0},{4,2},{6,4},{8,6},{10,8},{12,10},{14,12},{16,14},{18,... | collective-permute-start | bytes 3145736 | tf_op jit(solution)/shard_map/ppermute | solution.py:106
  23.3 17.3 %collective-permute-done.2.refs_9_.refs_12_.refs_14_.refs_16_.refs_18_.refs_1_ = bf16[512,1024]{1,0:T(8,128)(2,1)S(1)} collective-permute-done((bf16[512,1024]{1,0:T(8,128)(2,1)}, bf16[512,1024]{1,0:T(8,128)(2,1)S(1)}, u32[]{:S(2)}, u32[]{:S(2)}) %collective-permute-start.2) | collective-permute-done | bytes 1048608 | tf_op jit(solution)/shard_map/ppermute | solution.py:106
  45.6 3.7 collective-permute-start.4
  54.7 15.0 %all-reduce.table = s32[512]{0:T(512)} all-reduce(s32[512]{0:T(512)S(1)} %dynamic-update-slice), channel_id=1, replica_groups=mesh['ind'=16,'z'=16,'core'=2] {'z'}, use_global_device_ids=true, to_apply=%add | all-reduce | flops 512 | bytes 4096
  71.2 7.3 %shard_map.46 = bf16[16,10,2,16,256]{4,3,2,1,0:T(8,128)(2,1)} custom-call(s32[512]{0:T(512)} %all-reduce.table, s32[2]{0:T(128)} %pad_add_fusion.place, f32[512,1]{1,0:T(8,128)} %copy.26.residual, bf16[512,1024]{1,0:T(8,128)(2,1)} %refs_13_.1, bf16[512,1024]{1,0:T(8,128)(2,1)} %refs_13_.1, bf16[512,1024]{1,0:T(8,128)(2,1)} %refs_13_.1, ...), custom_call_target="tpu_custom_call" | custom-call | flops 1342177280 | bytes 7864320 | tf_op jit(solution)/shard_map/pallas_call | solution.py:66
  78.5 3.5 copy.27
  83.3 3.9 collective-permute-start.7
  89.2 18.3 %collective-permute-done.7.refs_5_.refs_8_.refs_10_.refs_12_.refs_14_.refs_1_ = bf16[512,1024]{1,0:T(8,128)(2,1)S(1)} collective-permute-done((bf16[512,1024]{1,0:T(8,128)(2,1)S(1)}, bf16[512,1024]{1,0:T(8,128)(2,1)S(1)}, u32[]{:S(2)}, u32[]{:S(2)}) %collective-permute-start.7) | collective-permute-done | bytes 1048608 | tf_op jit(solution)/shard_map/ppermute | solution.py:106
  107.4 5.2 %collective-permute-start.8 = (bf16[512,1024]{1,0:T(8,128)(2,1)S(1)}, bf16[512,1024]{1,0:T(8,128)(2,1)S(1)}, u32[]{:S(2)}, u32[]{:S(2)}) collective-permute-start(bf16[512,1024]{1,0:T(8,128)(2,1)S(1)} %collective-permute-done.7.refs_5_.refs_8_.refs_10_.refs_12_.refs_14_.refs_1_), channel_id=1, source_target_pairs={{0,1},{1,0},{2,3},{3,2},{4,5},{5,4},{6,7},{7,6},{8,9},{9,8},{10,11... | collective-permute-start | bytes 3145736 | tf_op jit(solution)/shard_map/ppermute | solution.py:109
  112.7 5.2 %collective-permute-start.9 = (bf16[512,1024]{1,0:T(8,128)(2,1)S(1)}, bf16[512,1024]{1,0:T(8,128)(2,1)S(1)}, u32[]{:S(2)}, u32[]{:S(2)}) collective-permute-start(bf16[512,1024]{1,0:T(8,128)(2,1)S(1)} %collective-permute-done.6.refs_0_.refs_2_.refs_4_.refs_6_.refs_13_.refs_9_), channel_id=1, source_target_pairs={{0,1},{1,0},{2,3},{3,2},{4,5},{5,4},{6,7},{7,6},{8,9},{9,8},{10,11... | collective-permute-start | bytes 3145736 | tf_op jit(solution)/shard_map/ppermute | solution.py:109
  121.1 6.6 %shard_map.47 = bf16[16,8,2,16,256]{4,3,2,1,0:T(8,128)(2,1)} custom-call(s32[512]{0:T(512)} %all-reduce.table, s32[2]{0:T(128)} %pad_add_fusion.place, f32[512,1]{1,0:T(8,128)} %copy.26.residual, bf16[512,1024]{1,0:T(8,128)(2,1)} %copy-done.6, bf16[512,1024]{1,0:T(8,128)(2,1)} %copy-done, bf16[512,1024]{1,0:T(8,128)(2,1)} %copy-done.6, ...), custom_call_target="tpu_custom_call" | custom-call | flops 1073741824 | bytes 6291456 | tf_op jit(solution)/shard_map/pallas_call | solution.py:66
  137.4 20.9 %collective-permute-done.12.refs_5_.refs_8_.refs_10_.refs_12_.refs_14_.refs_1_ = bf16[512,1024]{1,0:T(8,128)(2,1)S(1)} collective-permute-done((bf16[512,1024]{1,0:T(8,128)(2,1)S(1)}, bf16[512,1024]{1,0:T(8,128)(2,1)S(1)}, u32[]{:S(2)}, u32[]{:S(2)}) %collective-permute-start.12) | collective-permute-done | bytes 1048608 | tf_op jit(solution)/shard_map/ppermute | solution.py:106
  168.3 5.5 %shard_map.48 = bf16[16,8,2,16,256]{4,3,2,1,0:T(8,128)(2,1)} custom-call(s32[512]{0:T(512)} %all-reduce.table, s32[2]{0:T(128)} %pad_add_fusion.place, f32[512,1]{1,0:T(8,128)} %copy.26.residual, bf16[512,1024]{1,0:T(8,128)(2,1)} %copy-done.10, bf16[512,1024]{1,0:T(8,128)(2,1)} %copy-done.4, bf16[512,1024]{1,0:T(8,128)(2,1)} %copy-done.10, ...), custom_call_target="tpu_custom_call" | custom-call | flops 1073741824 | bytes 6291456 | tf_op jit(solution)/shard_map/pallas_call | solution.py:66
  178.3 3.9 collective-permute-start.17
  184.1 20.4 %collective-permute-done.17.refs_5_.refs_8_.refs_10_ = bf16[512,1024]{1,0:T(8,128)(2,1)S(1)} collective-permute-done((bf16[512,1024]{1,0:T(8,128)(2,1)S(1)}, bf16[512,1024]{1,0:T(8,128)(2,1)S(1)}, u32[]{:S(2)}, u32[]{:S(2)}) %collective-permute-start.17) | collective-permute-done | bytes 1048608 | tf_op jit(solution)/shard_map/ppermute | solution.py:106
  211.8 4.8 %shard_map.49 = bf16[16,6,2,16,256]{4,3,2,1,0:T(8,128)(2,1)} custom-call(s32[512]{0:T(512)} %all-reduce.table, s32[2]{0:T(128)} %pad_add_fusion.place, f32[512,1]{1,0:T(8,128)} %copy.26.residual, bf16[512,1024]{1,0:T(8,128)(2,1)} %copy-done.12, bf16[512,1024]{1,0:T(8,128)(2,1)} %copy-done.8, bf16[512,1024]{1,0:T(8,128)(2,1)} %copy-done.12, ...), custom_call_target="tpu_custom_call" | custom-call | flops 805306368 | bytes 4718592 | tf_op jit(solution)/shard_map/pallas_call | solution.py:66
  217.6 4.0 collective-permute-start.5
  221.6 42.6 %reduce-scatter.15.cloned.1.call-done = bf16[1,8,2,16,256]{4,3,1,2,0:T(8,128)(2,1)} async-done(((bf16[16,8,2,16,256]{4,3,1,2,0:T(8,128)(2,1)}), bf16[1,8,2,16,256]{4,3,1,2,0:T(8,128)(2,1)}) %reduce-scatter.15.cloned.1.call-update) | async-done | bytes 131088
  265.2 6.5 %collective-permute-start.10 = (bf16[4,16,256]{2,1,0:T(8,128)(2,1)S(1)}, bf16[4,16,256]{2,1,0:T(8,128)(2,1)S(1)}, u32[]{:S(2)}, u32[]{:S(2)}) collective-permute-start(bf16[4,16,256]{2,1,0:T(8,128)(2,1)S(1)} %get-tuple-element.12), channel_id=1, source_target_pairs={{0,28},{2,30},{4,0},{6,2},{8,4},{10,6},{12,8},{14,10},{16,12},{18,... | collective-permute-start | bytes 98312 | tf_op jit(solution)/shard_map/ppermute | solution.py:106
  276.0 82.4 %reduce-scatter.17.cloned.1.call-done = bf16[1,8,2,16,256]{4,3,1,2,0:T(8,128)(2,1)} async-done(((bf16[16,8,2,16,256]{4,3,1,2,0:T(8,128)(2,1)}), bf16[1,8,2,16,256]{4,3,1,2,0:T(8,128)(2,1)}) %reduce-scatter.17.cloned.1.call-update) | async-done | bytes 131088
  359.3 7.3 %collective-permute-start.15 = (bf16[4,16,256]{2,1,0:T(8,128)(2,1)S(1)}, bf16[4,16,256]{2,1,0:T(8,128)(2,1)S(1)}, u32[]{:S(2)}, u32[]{:S(2)}) collective-permute-start(bf16[4,16,256]{2,1,0:T(8,128)(2,1)S(1)} %get-tuple-element.14), channel_id=1, source_target_pairs={{0,26},{2,28},{4,30},{6,0},{8,2},{10,4},{12,6},{14,8},{16,10},{18,... | collective-permute-start | bytes 98312 | tf_op jit(solution)/shard_map/ppermute | solution.py:106
  366.6 85.0 %reduce-scatter.19.cloned.1.call-done = bf16[1,6,2,16,256]{4,3,2,1,0:T(8,128)(2,1)} async-done(((bf16[16,6,2,16,256]{4,3,2,1,0:T(8,128)(2,1)}), bf16[1,6,2,16,256]{4,3,2,1,0:T(8,128)(2,1)}) %reduce-scatter.19.cloned.1.call-update) | async-done | bytes 98320
  452.6 8.1 %collective-permute-start.19 = (bf16[4,16,256]{2,1,0:T(8,128)(2,1)S(1)}, bf16[4,16,256]{2,1,0:T(8,128)(2,1)S(1)}, u32[]{:S(2)}, u32[]{:S(2)}) collective-permute-start(bf16[4,16,256]{2,1,0:T(8,128)(2,1)S(1)} %slice_bitcast_fusion.3), channel_id=1, source_target_pairs={{0,24},{2,26},{4,28},{6,30},{8,0},{10,2},{12,4},{14,6},{16,8},{18,... | collective-permute-start | bytes 98312 | tf_op jit(solution)/shard_map/ppermute | solution.py:106
  462.7 4.4 collective-permute-start.21
  (123 shorter events, 69.7 us)
Async XLA Ops:
  6.5 210.1 %reduce-scatter.13.cloned.1.call-start = ((), (), s32[]{:S(2)}) async-start(), calls=%async_computation.4 | async-start | bytes 2785280
  6.5 34.1 %collective-permute-start.2 = (bf16[512,1024]{1,0:T(8,128)(2,1)}, bf16[512,1024]{1,0:T(8,128)(2,1)S(1)}, u32[]{:S(2)}, u32[]{:S(2)}) collective-permute-start(bf16[512,1024]{1,0:T(8,128)(2,1)} %refs_13_.1), channel_id=1, source_target_pairs={{0,30},{2,0},{4,2},{6,4},{8,6},{10,8},{12,10},{14,12},{16,14},{18,... | collective-permute-start | bytes 3145736 | tf_op jit(solution)/shard_map/ppermute | solution.py:106
  18.5 27.1 %collective-permute-start.1 = (bf16[512,1024]{1,0:T(8,128)(2,1)}, bf16[512,1024]{1,0:T(8,128)(2,1)S(1)}, u32[]{:S(2)}, u32[]{:S(2)}) collective-permute-start(bf16[512,1024]{1,0:T(8,128)(2,1)} %refs_13_.1), channel_id=1, source_target_pairs={{0,2},{2,4},{4,6},{6,8},{8,10},{10,12},{12,14},{14,16},{16,18},{18... | collective-permute-start | bytes 3145736 | tf_op jit(solution)/shard_map/ppermute | solution.py:106
  20.4 49.8 %collective-permute-start = (bf16[512,1024]{1,0:T(8,128)(2,1)}, bf16[512,1024]{1,0:T(8,128)(2,1)S(1)}, u32[]{:S(2)}, u32[]{:S(2)}) collective-permute-start(bf16[512,1024]{1,0:T(8,128)(2,1)} %refs_13_.1), channel_id=1, source_target_pairs={{0,1},{1,0},{2,3},{3,2},{4,5},{5,4},{6,7},{7,6},{8,9},{9,8},{10,11... | collective-permute-start | bytes 3145736 | tf_op jit(solution)/shard_map/ppermute | solution.py:109
  40.6 29.6 %collective-permute-start.3 = (bf16[512,1024]{1,0:T(8,128)(2,1)S(1)}, bf16[512,1024]{1,0:T(8,128)(2,1)}, u32[]{:S(2)}, u32[]{:S(2)}) collective-permute-start(bf16[512,1024]{1,0:T(8,128)(2,1)S(1)} %collective-permute-done.2.refs_9_.refs_12_.refs_14_.refs_16_.refs_18_.refs_1_), channel_id=1, source_target_pairs={{0,1},{1,0},{2,3},{3,2},{4,5},{5,4},{6,7},{7,6},{8,9},{9,8},{10,11... | collective-permute-start | bytes 3145736 | tf_op jit(solution)/shard_map/ppermute | solution.py:109
  45.6 24.7 %collective-permute-start.4 = (bf16[512,1024]{1,0:T(8,128)(2,1)S(1)}, bf16[512,1024]{1,0:T(8,128)(2,1)}, u32[]{:S(2)}, u32[]{:S(2)}) collective-permute-start(bf16[512,1024]{1,0:T(8,128)(2,1)S(1)} %collective-permute-done.1.refs_4_.refs_6_.refs_8_.refs_10_.refs_17_.refs_9_), channel_id=1, source_target_pairs={{0,1},{1,0},{2,3},{3,2},{4,5},{5,4},{6,7},{7,6},{8,9},{9,8},{10,11... | collective-permute-start | bytes 3145736 | tf_op jit(solution)/shard_map/ppermute | solution.py:109
  82.1 182.2 %reduce-scatter.15.cloned.1.call-start = ((), (), s32[]{:S(2)}) async-start(), calls=%async_computation.5 | async-start | bytes 2228224
  83.3 24.2 %collective-permute-start.7 = (bf16[512,1024]{1,0:T(8,128)(2,1)S(1)}, bf16[512,1024]{1,0:T(8,128)(2,1)S(1)}, u32[]{:S(2)}, u32[]{:S(2)}) collective-permute-start(bf16[512,1024]{1,0:T(8,128)(2,1)S(1)} %copy-done.1), channel_id=1, source_target_pairs={{0,30},{2,0},{4,2},{6,4},{8,6},{10,8},{12,10},{14,12},{16,14},{18,... | collective-permute-start | bytes 3145736 | tf_op jit(solution)/shard_map/ppermute | solution.py:106
  87.2 25.4 %collective-permute-start.6 = (bf16[512,1024]{1,0:T(8,128)(2,1)S(1)}, bf16[512,1024]{1,0:T(8,128)(2,1)S(1)}, u32[]{:S(2)}, u32[]{:S(2)}) collective-permute-start(bf16[512,1024]{1,0:T(8,128)(2,1)S(1)} %copy-done.3), channel_id=1, source_target_pairs={{0,2},{2,4},{4,6},{6,8},{8,10},{10,12},{12,14},{14,16},{16,18},{18... | collective-permute-start | bytes 3145736 | tf_op jit(solution)/shard_map/ppermute | solution.py:106
  107.4 10.4 %collective-permute-start.8 = (bf16[512,1024]{1,0:T(8,128)(2,1)S(1)}, bf16[512,1024]{1,0:T(8,128)(2,1)S(1)}, u32[]{:S(2)}, u32[]{:S(2)}) collective-permute-start(bf16[512,1024]{1,0:T(8,128)(2,1)S(1)} %collective-permute-done.7.refs_5_.refs_8_.refs_10_.refs_12_.refs_14_.refs_1_), channel_id=1, source_target_pairs={{0,1},{1,0},{2,3},{3,2},{4,5},{5,4},{6,7},{7,6},{8,9},{9,8},{10,11... | collective-permute-start | bytes 3145736 | tf_op jit(solution)/shard_map/ppermute | solution.py:109
  130.9 227.5 %reduce-scatter.17.cloned.1.call-start = ((), (), s32[]{:S(2)}) async-start(), calls=%async_computation.6 | async-start | bytes 2228224
  132.1 26.2 %collective-permute-start.12 = (bf16[512,1024]{1,0:T(8,128)(2,1)S(1)}, bf16[512,1024]{1,0:T(8,128)(2,1)S(1)}, u32[]{:S(2)}, u32[]{:S(2)}) collective-permute-start(bf16[512,1024]{1,0:T(8,128)(2,1)S(1)} %copy-done.5), channel_id=1, source_target_pairs={{0,30},{2,0},{4,2},{6,4},{8,6},{10,8},{12,10},{14,12},{16,14},{18,... | collective-permute-start | bytes 3145736 | tf_op jit(solution)/shard_map/ppermute | solution.py:106
  134.4 27.3 %collective-permute-start.11 = (bf16[512,1024]{1,0:T(8,128)(2,1)S(1)}, bf16[512,1024]{1,0:T(8,128)(2,1)S(1)}, u32[]{:S(2)}, u32[]{:S(2)}) collective-permute-start(bf16[512,1024]{1,0:T(8,128)(2,1)S(1)} %copy-done.7), channel_id=1, source_target_pairs={{0,2},{2,4},{4,6},{6,8},{8,10},{10,12},{12,14},{14,16},{16,18},{18... | collective-permute-start | bytes 3145736 | tf_op jit(solution)/shard_map/ppermute | solution.py:106
  177.1 274.6 %reduce-scatter.19.cloned.1.call-start = ((), (), s32[]{:S(2)}) async-start(), calls=%async_computation.7 | async-start | bytes 1671168
  178.3 26.2 %collective-permute-start.17 = (bf16[512,1024]{1,0:T(8,128)(2,1)S(1)}, bf16[512,1024]{1,0:T(8,128)(2,1)S(1)}, u32[]{:S(2)}, u32[]{:S(2)}) collective-permute-start(bf16[512,1024]{1,0:T(8,128)(2,1)S(1)} %copy-done.9), channel_id=1, source_target_pairs={{0,30},{2,0},{4,2},{6,4},{8,6},{10,8},{12,10},{14,12},{16,14},{18,... | collective-permute-start | bytes 3145736 | tf_op jit(solution)/shard_map/ppermute | solution.py:106
  182.2 27.6 %collective-permute-start.16 = (bf16[512,1024]{1,0:T(8,128)(2,1)S(1)}, bf16[512,1024]{1,0:T(8,128)(2,1)S(1)}, u32[]{:S(2)}, u32[]{:S(2)}) collective-permute-start(bf16[512,1024]{1,0:T(8,128)(2,1)S(1)} %copy-done.11), channel_id=1, source_target_pairs={{0,2},{2,4},{4,6},{6,8},{8,10},{10,12},{12,14},{14,16},{16,18},{18... | collective-permute-start | bytes 3145736 | tf_op jit(solution)/shard_map/ppermute | solution.py:106
  217.6 58.3 %collective-permute-start.5 = (bf16[4,16,256]{2,1,0:T(8,128)(2,1)S(1)}, bf16[4,16,256]{2,1,0:T(8,128)(2,1)S(1)}, u32[]{:S(2)}, u32[]{:S(2)}) collective-permute-start(bf16[4,16,256]{2,1,0:T(8,128)(2,1)S(1)} %get-tuple-element.10), channel_id=1, source_target_pairs={{0,30},{2,0},{4,2},{6,4},{8,6},{10,8},{12,10},{14,12},{16,14},{18,... | collective-permute-start | bytes 98312 | tf_op jit(solution)/shard_map/ppermute | solution.py:106
  265.2 10.7 %collective-permute-start.10 = (bf16[4,16,256]{2,1,0:T(8,128)(2,1)S(1)}, bf16[4,16,256]{2,1,0:T(8,128)(2,1)S(1)}, u32[]{:S(2)}, u32[]{:S(2)}) collective-permute-start(bf16[4,16,256]{2,1,0:T(8,128)(2,1)S(1)} %get-tuple-element.12), channel_id=1, source_target_pairs={{0,28},{2,30},{4,0},{6,2},{8,4},{10,6},{12,8},{14,10},{16,12},{18,... | collective-permute-start | bytes 98312 | tf_op jit(solution)/shard_map/ppermute | solution.py:106
  271.7 198.7 %collective-permute-start.22 = (bf16[4,16,256]{2,1,0:T(8,128)(2,1)S(1)}, bf16[4,16,256]{2,1,0:T(8,128)(2,1)S(1)}, u32[]{:S(2)}, u32[]{:S(2)}) collective-permute-start(bf16[4,16,256]{2,1,0:T(8,128)(2,1)S(1)} %get-tuple-element.11), channel_id=1, source_target_pairs={{0,4},{2,6},{4,8},{6,10},{8,12},{10,14},{12,16},{14,18},{16,20},{1... | collective-permute-start | bytes 98312 | tf_op jit(solution)/shard_map/ppermute | solution.py:106
  273.6 196.8 %collective-permute-start.23 = (bf16[4,16,256]{2,1,0:T(8,128)(2,1)S(1)}, bf16[4,16,256]{2,1,0:T(8,128)(2,1)S(1)}, u32[]{:S(2)}, u32[]{:S(2)}) collective-permute-start(bf16[4,16,256]{2,1,0:T(8,128)(2,1)S(1)} %get-tuple-element.9), channel_id=1, source_target_pairs={{0,2},{2,4},{4,6},{6,8},{8,10},{10,12},{12,14},{14,16},{16,18},{18... | collective-permute-start | bytes 98312 | tf_op jit(solution)/shard_map/ppermute | solution.py:106
  359.3 103.3 %collective-permute-start.15 = (bf16[4,16,256]{2,1,0:T(8,128)(2,1)S(1)}, bf16[4,16,256]{2,1,0:T(8,128)(2,1)S(1)}, u32[]{:S(2)}, u32[]{:S(2)}) collective-permute-start(bf16[4,16,256]{2,1,0:T(8,128)(2,1)S(1)} %get-tuple-element.14), channel_id=1, source_target_pairs={{0,26},{2,28},{4,30},{6,0},{8,2},{10,4},{12,6},{14,8},{16,10},{18,... | collective-permute-start | bytes 98312 | tf_op jit(solution)/shard_map/ppermute | solution.py:106
  452.6 14.5 %collective-permute-start.19 = (bf16[4,16,256]{2,1,0:T(8,128)(2,1)S(1)}, bf16[4,16,256]{2,1,0:T(8,128)(2,1)S(1)}, u32[]{:S(2)}, u32[]{:S(2)}) collective-permute-start(bf16[4,16,256]{2,1,0:T(8,128)(2,1)S(1)} %slice_bitcast_fusion.3), channel_id=1, source_target_pairs={{0,24},{2,26},{4,28},{6,30},{8,0},{10,2},{12,4},{14,6},{16,8},{18,... | collective-permute-start | bytes 98312 | tf_op jit(solution)/shard_map/ppermute | solution.py:106
  460.7 8.4 %collective-permute-start.20 = (bf16[2,16,256]{2,1,0:T(8,128)(2,1)S(1)}, bf16[2,16,256]{2,1,0:T(8,128)(2,1)S(1)}, u32[]{:S(2)}, u32[]{:S(2)}) collective-permute-start(bf16[2,16,256]{2,1,0:T(8,128)(2,1)S(1)} %slice_bitcast_fusion.7), channel_id=1, source_target_pairs={{0,8},{2,10},{4,12},{6,14},{8,16},{10,18},{12,20},{14,22},{16,24},... | collective-permute-start | bytes 49160 | tf_op jit(solution)/shard_map/ppermute | solution.py:106
  462.7 7.8 %collective-permute-start.21 = (bf16[4,16,256]{2,1,0:T(8,128)(2,1)S(1)}, bf16[4,16,256]{2,1,0:T(8,128)(2,1)S(1)}, u32[]{:S(2)}, u32[]{:S(2)}) collective-permute-start(bf16[4,16,256]{2,1,0:T(8,128)(2,1)S(1)} %get-tuple-element.13), channel_id=1, source_target_pairs={{0,6},{2,8},{4,10},{6,12},{8,14},{10,16},{12,18},{14,20},{16,22},{... | collective-permute-start | bytes 98312 | tf_op jit(solution)/shard_map/ppermute | solution.py:106
  (24 other events, 141.9 us)
Sparse Core Ops, SparseCore 0:
  82.2 87.9 reduce-scatter.12
  174.3 89.8 reduce-scatter.14
  268.4 89.9 reduce-scatter.16
  362.3 89.2 reduce-scatter.18

commit v2 on v1

v2 whole, which is shorter than its diff:
```python
import functools

import jax
import jax.numpy as jnp
from jax import lax
from jax.experimental import pallas as pl
from jax.experimental.pallas import tpu as pltpu
from jax.sharding import Mesh
from jax.sharding import PartitionSpec as P

B = 256
EPSILON = 1e-05
RING = ("z", "core")


def entry_at(cell, ring, place):
    away, back, first_other, second_other = cell
    chip, core = place[0], place[1]
    sign = 1 - 2 * core
    owner = lax.rem(chip - sign * back + ring, ring)
    distance = lax.rem(sign * away + ring, ring)
    first = 1 - core if first_other else core
    second = 1 - core if second_other else core
    return ((owner * 2 + first) * ring + distance) * 2 + second


def tile_kernel(cells, where, ring, table, place, residual, *refs):
    out = refs[-1]
    parts = out.shape[0]
    depth = B // parts
    for j, (cell, (a_at, c_at)) in enumerate(zip(cells, where)):
        entry = table[entry_at(cell, ring, place)]
        rows = slice(2 * j * depth, 2 * (j + 1) * depth)

        @pl.when(entry > 0)
        def _(a_ref=refs[a_at], c_ref=refs[c_at], j=j, entry=entry):
            first = pl.multiple_of((entry - 1) // 4 * B, B)
            second = pl.multiple_of(lax.rem(entry - 1, 4) * B, B)
            left = a_ref[:, pl.ds(first, B)].astype(jnp.float32)
            weighted = (residual[...] * left).astype(jnp.bfloat16)
            right = c_ref[:, pl.ds(second, B)]
            over_rows = (((0,), (0,)), ((), ()))
            cross = lax.dot_general(
                weighted, right, over_rows, preferred_element_type=jnp.float32
            )
            spread = lax.dot_general(
                weighted * weighted, right * right, over_rows, preferred_element_type=jnp.float32
            )
            cross = cross.astype(jnp.bfloat16).reshape(parts, depth, B)
            spread = spread.astype(jnp.bfloat16).reshape(parts, depth, B)
            out[:, 2 * j * depth : (2 * j + 1) * depth, :] = cross
            out[:, (2 * j + 1) * depth : (2 * j + 2) * depth, :] = spread

        @pl.when(entry == 0)
        def _(rows=rows):
            out[:, rows, :] = jnp.zeros((parts, 2 * depth, B), jnp.bfloat16)


def tiles(cells, operands, ring, parts, table, place, residual):
    arrays, where = [], []
    for pair in operands:
        spots = []
        for x in pair:
            spot = next((i for i, y in enumerate(arrays) if y is x), len(arrays))
            if spot == len(arrays):
                arrays.append(x)
            spots.append(spot)
        where.append(tuple(spots))
    rows = residual.shape[0]
    shape = (parts, len(cells) * 2 * (B // parts), B)
    smem = pl.BlockSpec(memory_space=pltpu.SMEM)
    vmem = pl.BlockSpec(memory_space=pltpu.VMEM)
    return pl.pallas_call(
        functools.partial(tile_kernel, cells, where, ring),
        out_shape=jax.ShapeDtypeStruct(shape, jnp.bfloat16),
        in_specs=[smem, smem, vmem] + [vmem] * len(arrays),
        out_specs=vmem,
        cost_estimate=pl.CostEstimate(
            flops=len(cells) * 4 * rows * B * B,
            bytes_accessed=len(cells) * (2 * rows * B * 2 + 2 * B * B * 2),
            transcendentals=0,
        ),
        compiler_params=pltpu.CompilerParams(vmem_limit_bytes=24 << 20),
    )(table, place, residual, *arrays)


def on_device(dosage, residual, pairs, counts):
    ring = lax.axis_size("z")
    parts = lax.axis_size("ind")
    chip, core = lax.axis_index("z"), lax.axis_index("core")
    total_rows = dosage.shape[0] * parts
    local_blocks = dosage.shape[1] // B
    slot_count = pairs.shape[0]
    depth = B // parts

    def move(x, by, cross=False):
        perm = []
        for z in range(ring):
            for k in range(2):
                to = (z + (by if k == 0 else -by)) % ring
                perm.append((z * 2 + k, to * 2 + (1 - k if cross else k)))
        return lax.ppermute(x, RING, perm)

    def swap(x):
        return move(x, 0, True)

    live = jnp.arange(slot_count, dtype=jnp.int32) < counts[0]
    first_local = pairs[:, 0] - (chip * 2 + core) * local_blocks
    second_local = pairs[:, 1] % local_blocks
    holder = pairs[:, 1] // local_blocks
    away = (holder // 2 - chip) % ring
    position = away * 2 + holder % 2
    wanted = (position[:, None] == jnp.arange(2 * ring, dtype=jnp.int32)[None, :]) & live[:, None]
    code = 1 + first_local * local_blocks + second_local
    row = jnp.sum(jnp.where(wanted, code[:, None], 0), axis=0)
    rows = jnp.broadcast_to(row[None, :], (2 * ring, 2 * ring))
    table = lax.all_to_all(rows, RING, 0, 0, tiled=True).reshape(-1)
    place = jnp.stack([chip, core]).astype(jnp.int32)
    column = residual[:, None]

    hops = ring // 4
    own, other = [dosage], [swap(dosage)]
    far_own, far_other = [dosage], [other[0]]
    near, cross = {}, {}
    for h in range(0, hops + 1):
        cells, operands = [], []
        if h == 0:
            cells = [(0, 0, False, False), (0, 0, False, True)]
            operands = [(dosage, dosage), (dosage, other[0])]
        else:
            own.append(move(own[h - 1], 1))
            other.append(move(other[h - 1], 1))
            far_other.append(swap(own[h]))
            far_own.append(swap(other[h]))
            for first_other in (False, True):
                a = other[h] if first_other else own[h]
                for away_by, at in ((2 * h - 1, h - 1), (2 * h, h)):
                    if away_by == 2 * hops and first_other:
                        continue
                    for second_other in (False, True):
                        c = far_other[at] if second_other else far_own[at]
                        cells.append((away_by, h, first_other, second_other))
                        operands.append((a, c))
        partial = tiles(tuple(cells), operands, ring, parts, table, place, column)
        arrived = lax.all_to_all(partial, "ind", 0, 0, tiled=True)
        summed = jnp.sum(arrived.astype(jnp.float32), axis=0)
        summed = summed.reshape(len(cells), 2, depth, B)
        scores = summed[:, 0] / jnp.sqrt(summed[:, 1] + EPSILON * total_rows)
        scores = scores.astype(jnp.bfloat16)
        if h == 0:
            near[0] = scores
            continue
        near[h] = move(scores[:4], -h)
        cross[h] = move(scores[4:], -h, True)
    found = jnp.concatenate(
        [near[h] for h in range(hops + 1)]
        + [jnp.concatenate([cross[h][2:4], cross[h][0:2]]) if h < hops else cross[h][0:2] for h in range(hops, 0, -1)],
        axis=0,
    )
    ahead = jnp.where(core == 0, away, -away) % ring
    unlike = (holder % 2 != core).astype(jnp.int32)
    index = ahead * 2 + jnp.where(ahead <= 2 * hops, unlike, 1 - unlike)
    picked = jnp.take(found, index, axis=0)
    picked = jnp.where(live[:, None, None], picked, jnp.bfloat16(0.0))
    return jnp.transpose(picked, (1, 0, 2))


def solution(mesh):
    devices = mesh.devices.reshape(mesh.shape["ind"], mesh.shape["blk"] // 2, 2)
    torus = Mesh(devices, ("ind", *RING))
    placed = (P("ind", RING), P("ind"), P(RING, None), P(RING))
    return jax.shard_map(
        on_device, mesh=torus, in_specs=placed, out_specs=P("ind", RING, None), check_vma=False
    )
```

time: 482 us -> 241 us (0.50)
  waiting for transfers between devices: 299 us -> 55.4 us
  starting transfers between devices: 97.4 us -> 148 us
  blocking collectives: 15 us -> 0 us
  local copies, waits for them, and re-layouts: 22.7 us -> 8.58 us
  between operations: 15.1 us -> 1.27 us
  Pallas kernels: 24.2 us -> 19.1 us
    unnamed x8 -> x0, waiting for transfers between devices: 210 us -> none
    ppermute x24 -> x25, waiting for transfers between devices: 88.6 us -> 38.5 us  [move(): return lax.ppermute(x, RING, perm)]
    all_to_all x0 -> x6, starting transfers between devices: none -> 43.4 us  [the longest x5 34.3 us: on_device(): arrived = lax.all_to_all(partial, 'ind', 0, 0, tiled=True)]
    all_to_all x0 -> x6, waiting for transfers between devices: none -> 16.9 us  [the longest x1 10.8 us: on_device(): table = lax.all_to_all(rows, RING, 0, 0, tiled=True).reshape(-1)]
    unnamed x1 -> x0, blocking collectives: 15 us -> none
    pallas_call x3 -> x0, local copies, waits for them, and re-layouts: 10 us -> none  [tiles(): pl.pallas_call(functools.partial(tile_kernel, cells, ring), out_shape=jax...]
    reduce_sum x0 -> x5, other arithmetic: none -> 7.05 us  [on_device(): summed = jnp.sum(arrived.astype(jnp.float32), axis=0)]
    ppermute x24 -> x25, starting transfers between devices: 97.3 us -> 104 us  [move(): return lax.ppermute(x, RING, perm)]
  transfers between devices with their start and end apart: 28 -> 31, of which waited for: 15 -> 11; matrix products, arithmetic and copies ran while one was open for 3% -> 5% of each run, Pallas kernels for 4% -> 8%
where the time goes in v2:
time: 241 us; the launch traced here: 242 us
  starting transfers between devices  148 us (61%)
  waiting for transfers between devices  55.4 us (23%)
  Pallas kernels  19.1 us (8%)
  other arithmetic  9.63 us (4%)
  local copies, waits for them, and re-layouts  8.58 us (4%)
    ppermute x25, starting transfers between devices, move(): return lax.ppermute(x, RING, perm)  104 us
    ppermute x25, waiting for transfers between devices, move(): return lax.ppermute(x, RING, perm)  38.5 us
    all_to_all x5, starting transfers between devices, on_device(): arrived = lax.all_to_all(partial, 'ind', 0, 0, tiled=True)  34.3 us
    pallas_call x5, Pallas kernels, tiles(): pl.pallas_call(functools.partial(tile_kernel, cells, where, ring), out_sh...  19.1 us
    all_to_all x1, waiting for transfers between devices, on_device(): table = lax.all_to_all(rows, RING, 0, 0, tiled=True).reshape(-1)  10.8 us
    all_to_all x1, starting transfers between devices, on_device(): table = lax.all_to_all(rows, RING, 0, 0, tiled=True).reshape(-1)  9.09 us
    reduce_sum x5, other arithmetic, on_device(): summed = jnp.sum(arrived.astype(jnp.float32), axis=0)  7.05 us
    all_to_all x5, waiting for transfers between devices, on_device(): arrived = lax.all_to_all(partial, 'ind', 0, 0, tiled=True)  6.01 us
  transfers between devices with their start and end apart: 31, of which 11 were waited for; matrix products, arithmetic and copies ran while one was open for 5% of the time, Pallas kernels for 8%

profile of v2, /device:TPU:1, one launch (start us, length us, event | category | flops | bytes accessed | tf_op | source)
XLA Modules:
  0.0 241.6 jit_solution(8302607397401112803)
XLA Ops:
  0.0 8.7 %collective-permute-start = (bf16[512,1024]{1,0:T(8,128)(2,1)}, bf16[512,1024]{1,0:T(8,128)(2,1)S(1)}, u32[]{:S(2)}, u32[]{:S(2)}) collective-permute-start(bf16[512,1024]{1,0:T(8,128)(2,1)} %refs_1_.1), channel_id=1, source_target_pairs={{0,1},{1,0},{2,3},{3,2},{4,5},{5,4},{6,7},{7,6},{8,9},{9,8},{10,11... | collective-permute-start | bytes 3145736 | tf_op jit(solution)/shard_map/ppermute | solution.py:102
  8.7 5.8 %collective-permute-start.1 = (bf16[512,1024]{1,0:T(8,128)(2,1)}, bf16[512,1024]{1,0:T(8,128)(2,1)}, u32[]{:S(2)}, u32[]{:S(2)}) collective-permute-start(bf16[512,1024]{1,0:T(8,128)(2,1)} %refs_1_.1), channel_id=1, source_target_pairs={{0,2},{1,31},{2,4},{3,1},{4,6},{5,3},{6,8},{7,5},{8,10},{9,7},{10,... | collective-permute-start | bytes 3145736 | tf_op jit(solution)/shard_map/ppermute | solution.py:102
  17.9 8.7 %collective-permute-done.1.refs_0_ = bf16[512,1024]{1,0:T(8,128)(2,1)} collective-permute-done((bf16[512,1024]{1,0:T(8,128)(2,1)}, bf16[512,1024]{1,0:T(8,128)(2,1)}, u32[]{:S(2)}, u32[]{:S(2)}) %collective-permute-start.1) | collective-permute-done | bytes 1048608 | tf_op jit(solution)/shard_map/ppermute | solution.py:102
  29.8 7.9 %collective-permute-done.2.refs_5_ = bf16[512,1024]{1,0:T(8,128)(2,1)} collective-permute-done((bf16[512,1024]{1,0:T(8,128)(2,1)S(1)}, bf16[512,1024]{1,0:T(8,128)(2,1)}, u32[]{:S(2)}, u32[]{:S(2)}) %collective-permute-start.2) | collective-permute-done | bytes 1048608 | tf_op jit(solution)/shard_map/ppermute | solution.py:102
  43.3 9.1 %all-to-all-start = ((s32[32,1,32]{2,1,0:T(1,128)}), s32[32,1,32]{2,1,0:T(1,128)S(1)}, u32[]{:S(2)}, u32[]{:S(2)}) async-start(s32[32,1,32]{2,1,0:T(1,128)} %broadcast_in_dim.55), calls=%async_computation | async-start | bytes 32768 | tf_op jit(solution)/shard_map/all_to_all | solution.py:117
  53.3 10.8 %all-to-all-done = s32[32,1,32]{2,1,0:T(1,128)S(1)} async-done(((s32[32,1,32]{2,1,0:T(1,128)}), s32[32,1,32]{2,1,0:T(1,128)S(1)}, u32[]{:S(2)}, u32[]{:S(2)}) %all-to-all-start) | async-done | bytes 4128 | tf_op jit(solution)/shard_map/all_to_all | solution.py:117
  68.1 6.8 %all-to-all-start.1 = ((bf16[16,64,256]{2,1,0:T(8,128)(2,1)}), bf16[16,64,256]{2,1,0:T(8,128)(2,1)}, u32[]{:S(2)}, u32[]{:S(2)}) async-start(bf16[16,64,256]{2,1,0:T(8,128)(2,1)} %copy-done.6), calls=%async_computation.1 | async-start | bytes 1048576 | tf_op jit(solution)/shard_map/all_to_all | solution.py:145
  80.4 4.8 %shard_map.47 = bf16[16,256,256]{2,1,0:T(8,128)(2,1)} custom-call(s32[1024]{0:T(1024)S(1)} %reshape.70.table, s32[2]{0:T(128)S(1)} %pad_add_fusion.place, f32[512,1]{1,0:T(8,128)S(1)} %copy.34.residual, bf16[512,1024]{1,0:T(8,128)(2,1)} %collective-permute-done.1.refs_0_, bf16[512,1024]{1,0:T(8,128)(2,1)S(1)} %copy-done.1, ...), custom_call_target="tpu_custom_call" | custom-call | flops 1073741824 | bytes 6291456 | tf_op jit(solution)/shard_map/pallas_call | solution.py:73
  85.3 6.6 %all-to-all-start.2 = ((bf16[16,256,256]{2,1,0:T(8,128)(2,1)}), bf16[16,256,256]{2,1,0:T(8,128)(2,1)}, u32[]{:S(2)}, u32[]{:S(2)}) async-start(bf16[16,256,256]{2,1,0:T(8,128)(2,1)} %shard_map.47), calls=%async_computation.2 | async-start | bytes 4194304 | tf_op jit(solution)/shard_map/all_to_all | solution.py:145
  91.9 4.7 %collective-permute-start.9 = (bf16[512,1024]{1,0:T(8,128)(2,1)}, bf16[512,1024]{1,0:T(8,128)(2,1)S(1)}, u32[]{:S(2)}, u32[]{:S(2)}) collective-permute-start(bf16[512,1024]{1,0:T(8,128)(2,1)} %collective-permute-done.6.refs_0_), channel_id=1, source_target_pairs={{0,1},{1,0},{2,3},{3,2},{4,5},{5,4},{6,7},{7,6},{8,9},{9,8},{10,11... | collective-permute-start | bytes 3145736 | tf_op jit(solution)/shard_map/ppermute | solution.py:102
  96.7 5.6 %collective-permute-done.7.refs_5_ = bf16[512,1024]{1,0:T(8,128)(2,1)} collective-permute-done((bf16[512,1024]{1,0:T(8,128)(2,1)}, bf16[512,1024]{1,0:T(8,128)(2,1)}, u32[]{:S(2)}, u32[]{:S(2)}) %collective-permute-start.7) | collective-permute-done | bytes 1048608 | tf_op jit(solution)/shard_map/ppermute | solution.py:102
  102.3 5.6 %collective-permute-start.8 = (bf16[512,1024]{1,0:T(8,128)(2,1)}, bf16[512,1024]{1,0:T(8,128)(2,1)S(1)}, u32[]{:S(2)}, u32[]{:S(2)}) collective-permute-start(bf16[512,1024]{1,0:T(8,128)(2,1)} %collective-permute-done.7.refs_5_), channel_id=1, source_target_pairs={{0,1},{1,0},{2,3},{3,2},{4,5},{5,4},{6,7},{7,6},{8,9},{9,8},{10,11... | collective-permute-start | bytes 3145736 | tf_op jit(solution)/shard_map/ppermute | solution.py:102
  111.8 4.9 %shard_map.48 = bf16[16,256,256]{2,1,0:T(8,128)(2,1)} custom-call(s32[1024]{0:T(1024)S(1)} %reshape.70.table, s32[2]{0:T(128)S(1)} %pad_add_fusion.place, f32[512,1]{1,0:T(8,128)S(1)} %copy.34.residual, bf16[512,1024]{1,0:T(8,128)(2,1)} %collective-permute-done.6.refs_0_, bf16[512,1024]{1,0:T(8,128)(2,1)} %collective-permute-done.3.refs_3_.refs_1_, ...), custom_call_target="tpu_custom_call" | custom-call | flops 1073741824 | bytes 6291456 | tf_op jit(solution)/shard_map/pallas_call | solution.py:73
  118.7 7.1 %all-to-all-start.3 = ((bf16[16,256,256]{2,1,0:T(8,128)(2,1)}), bf16[16,256,256]{2,1,0:T(8,128)(2,1)}, u32[]{:S(2)}, u32[]{:S(2)}) async-start(bf16[16,256,256]{2,1,0:T(8,128)(2,1)} %shard_map.48), calls=%async_computation.3 | async-start | bytes 4194304 | tf_op jit(solution)/shard_map/all_to_all | solution.py:145
  125.8 4.0 %collective-permute-start.14 = (bf16[512,1024]{1,0:T(8,128)(2,1)}, bf16[512,1024]{1,0:T(8,128)(2,1)S(1)}, u32[]{:S(2)}, u32[]{:S(2)}) collective-permute-start(bf16[512,1024]{1,0:T(8,128)(2,1)} %collective-permute-done.11.refs_0_), channel_id=1, source_target_pairs={{0,1},{1,0},{2,3},{3,2},{4,5},{5,4},{6,7},{7,6},{8,9},{9,8},{10,11... | collective-permute-start | bytes 3145736 | tf_op jit(solution)/shard_map/ppermute | solution.py:102
  129.9 5.4 %collective-permute-done.12.refs_5_ = bf16[512,1024]{1,0:T(8,128)(2,1)} collective-permute-done((bf16[512,1024]{1,0:T(8,128)(2,1)}, bf16[512,1024]{1,0:T(8,128)(2,1)}, u32[]{:S(2)}, u32[]{:S(2)}) %collective-permute-start.12) | collective-permute-done | bytes 1048608 | tf_op jit(solution)/shard_map/ppermute | solution.py:102
  144.4 5.3 %shard_map.49 = bf16[16,256,256]{2,1,0:T(8,128)(2,1)} custom-call(s32[1024]{0:T(1024)S(1)} %reshape.70.table, s32[2]{0:T(128)S(1)} %pad_add_fusion.place, f32[512,1]{1,0:T(8,128)S(1)} %copy.34.residual, bf16[512,1024]{1,0:T(8,128)(2,1)} %collective-permute-done.11.refs_0_, bf16[512,1024]{1,0:T(8,128)(2,1)S(1)} %copy-done.5, bf16[512,1024]{1,0:T(8,128)(2,1)S(1)} %copy-done.3, ...), custom_call_target="tpu_custom_call" | custom-call | flops 1073741824 | bytes 6291456 | tf_op jit(solution)/shard_map/pallas_call | solution.py:73
  153.1 6.5 %all-to-all-start.4 = ((bf16[16,256,256]{2,1,0:T(8,128)(2,1)}), bf16[16,256,256]{2,1,0:T(8,128)(2,1)}, u32[]{:S(2)}, u32[]{:S(2)}) async-start(bf16[16,256,256]{2,1,0:T(8,128)(2,1)} %shard_map.49), calls=%async_computation.4 | async-start | bytes 4194304 | tf_op jit(solution)/shard_map/all_to_all | solution.py:145
  159.6 4.3 %collective-permute-start.19 = (bf16[512,1024]{1,0:T(8,128)(2,1)}, bf16[512,1024]{1,0:T(8,128)(2,1)S(1)}, u32[]{:S(2)}, u32[]{:S(2)}) collective-permute-start(bf16[512,1024]{1,0:T(8,128)(2,1)} %collective-permute-done.16.refs_0_), channel_id=1, source_target_pairs={{0,1},{1,0},{2,3},{3,2},{4,5},{5,4},{6,7},{7,6},{8,9},{9,8},{10,11... | collective-permute-start | bytes 3145736 | tf_op jit(solution)/shard_map/ppermute | solution.py:102
  166.7 4.0 %collective-permute-start.18 = (bf16[512,1024]{1,0:T(8,128)(2,1)}, bf16[512,1024]{1,0:T(8,128)(2,1)S(1)}, u32[]{:S(2)}, u32[]{:S(2)}) collective-permute-start(bf16[512,1024]{1,0:T(8,128)(2,1)} %collective-permute-done.17.refs_5_), channel_id=1, source_target_pairs={{0,1},{1,0},{2,3},{3,2},{4,5},{5,4},{6,7},{7,6},{8,9},{9,8},{10,11... | collective-permute-start | bytes 3145736 | tf_op jit(solution)/shard_map/ppermute | solution.py:102
  186.0 7.2 %all-to-all-start.5 = ((bf16[16,192,256]{2,1,0:T(8,128)(2,1)}), bf16[16,192,256]{2,1,0:T(8,128)(2,1)S(1)}, u32[]{:S(2)}, u32[]{:S(2)}) async-start(bf16[16,192,256]{2,1,0:T(8,128)(2,1)} %shard_map.50), calls=%async_computation.5 | async-start | bytes 3145728 | tf_op jit(solution)/shard_map/all_to_all | solution.py:145
  195.2 8.1 %collective-permute-start.10 = (bf16[4,16,256]{2,1,0:T(8,128)(2,1)S(1)}, bf16[4,16,256]{2,1,0:T(8,128)(2,1)S(1)}, u32[]{:S(2)}, u32[]{:S(2)}) collective-permute-start(bf16[4,16,256]{2,1,0:T(8,128)(2,1)S(1)} %get-tuple-element.12), channel_id=1, source_target_pairs={{0,28},{1,5},{2,30},{3,7},{4,0},{5,9},{6,2},{7,11},{8,4},{9,13},{1... | collective-permute-start | bytes 98312 | tf_op jit(solution)/shard_map/ppermute | solution.py:102
  216.4 14.8 %collective-permute-start.20 = (bf16[4,16,256]{2,1,0:T(8,128)(2,1)S(1)}, bf16[4,16,256]{2,1,0:T(8,128)(2,1)S(1)}, u32[]{:S(2)}, u32[]{:S(2)}) collective-permute-start(bf16[4,16,256]{2,1,0:T(8,128)(2,1)S(1)} %slice_bitcast_fusion.11), channel_id=1, source_target_pairs={{0,24},{1,9},{2,26},{3,11},{4,28},{5,13},{6,30},{7,15},{8,0},{9,17... | collective-permute-start | bytes 98312 | tf_op jit(solution)/shard_map/ppermute | solution.py:102
  231.2 5.6 %collective-permute-start.21 = (bf16[2,16,256]{2,1,0:T(8,128)(2,1)S(1)}, bf16[2,16,256]{2,1,0:T(8,128)(2,1)S(1)}, u32[]{:S(2)}, u32[]{:S(2)}) collective-permute-start(bf16[2,16,256]{2,1,0:T(8,128)(2,1)S(1)} %slice_bitcast_fusion.17), channel_id=1, source_target_pairs={{0,25},{1,8},{2,27},{3,10},{4,29},{5,12},{6,31},{7,14},{8,1},{9,16... | collective-permute-start | bytes 49160 | tf_op jit(solution)/shard_map/ppermute | solution.py:102
  (97 shorter events, 77.9 us)
Async XLA Ops:
  8.7 17.8 %collective-permute-start.1 = (bf16[512,1024]{1,0:T(8,128)(2,1)}, bf16[512,1024]{1,0:T(8,128)(2,1)}, u32[]{:S(2)}, u32[]{:S(2)}) collective-permute-start(bf16[512,1024]{1,0:T(8,128)(2,1)} %refs_1_.1), channel_id=1, source_target_pairs={{0,2},{1,31},{2,4},{3,1},{4,6},{5,3},{6,8},{7,5},{8,10},{9,7},{10,... | collective-permute-start | bytes 3145736 | tf_op jit(solution)/shard_map/ppermute | solution.py:102
  14.5 23.2 %collective-permute-start.2 = (bf16[512,1024]{1,0:T(8,128)(2,1)S(1)}, bf16[512,1024]{1,0:T(8,128)(2,1)}, u32[]{:S(2)}, u32[]{:S(2)}) collective-permute-start(bf16[512,1024]{1,0:T(8,128)(2,1)S(1)} %collective-permute-done.refs_1_.refs_2_), channel_id=1, source_target_pairs={{0,2},{1,31},{2,4},{3,1},{4,6},{5,3},{6,8},{7,5},{8,10},{9,7},{10,... | collective-permute-start | bytes 3145736 | tf_op jit(solution)/shard_map/ppermute | solution.py:102
  26.6 53.8 %collective-permute-start.4 = (bf16[512,1024]{1,0:T(8,128)(2,1)}, bf16[512,1024]{1,0:T(8,128)(2,1)S(1)}, u32[]{:S(2)}, u32[]{:S(2)}) collective-permute-start(bf16[512,1024]{1,0:T(8,128)(2,1)} %collective-permute-done.1.refs_0_), channel_id=1, source_target_pairs={{0,1},{1,0},{2,3},{3,2},{4,5},{5,4},{6,7},{7,6},{8,9},{9,8},{10,11... | collective-permute-start | bytes 3145736 | tf_op jit(solution)/shard_map/ppermute | solution.py:102
  37.7 42.7 %collective-permute-start.3 = (bf16[512,1024]{1,0:T(8,128)(2,1)}, bf16[512,1024]{1,0:T(8,128)(2,1)}, u32[]{:S(2)}, u32[]{:S(2)}) collective-permute-start(bf16[512,1024]{1,0:T(8,128)(2,1)} %collective-permute-done.2.refs_5_), channel_id=1, source_target_pairs={{0,1},{1,0},{2,3},{3,2},{4,5},{5,4},{6,7},{7,6},{8,9},{9,8},{10,11... | collective-permute-start | bytes 3145736 | tf_op jit(solution)/shard_map/ppermute | solution.py:102
  43.3 20.8 %all-to-all-start = ((s32[32,1,32]{2,1,0:T(1,128)}), s32[32,1,32]{2,1,0:T(1,128)S(1)}, u32[]{:S(2)}, u32[]{:S(2)}) async-start(s32[32,1,32]{2,1,0:T(1,128)} %broadcast_in_dim.55), calls=%async_computation | async-start | bytes 32768 | tf_op jit(solution)/shard_map/all_to_all | solution.py:117
  68.1 17.2 %all-to-all-start.1 = ((bf16[16,64,256]{2,1,0:T(8,128)(2,1)}), bf16[16,64,256]{2,1,0:T(8,128)(2,1)}, u32[]{:S(2)}, u32[]{:S(2)}) async-start(bf16[16,64,256]{2,1,0:T(8,128)(2,1)} %copy-done.6), calls=%async_computation.1 | async-start | bytes 1048576 | tf_op jit(solution)/shard_map/all_to_all | solution.py:145
  74.9 17.0 %collective-permute-start.6 = (bf16[512,1024]{1,0:T(8,128)(2,1)}, bf16[512,1024]{1,0:T(8,128)(2,1)}, u32[]{:S(2)}, u32[]{:S(2)}) collective-permute-start(bf16[512,1024]{1,0:T(8,128)(2,1)} %collective-permute-done.1.refs_0_), channel_id=1, source_target_pairs={{0,2},{1,31},{2,4},{3,1},{4,6},{5,3},{6,8},{7,5},{8,10},{9,7},{10,... | collective-permute-start | bytes 3145736 | tf_op jit(solution)/shard_map/ppermute | solution.py:102
  77.2 25.1 %collective-permute-start.7 = (bf16[512,1024]{1,0:T(8,128)(2,1)}, bf16[512,1024]{1,0:T(8,128)(2,1)}, u32[]{:S(2)}, u32[]{:S(2)}) collective-permute-start(bf16[512,1024]{1,0:T(8,128)(2,1)} %collective-permute-done.2.refs_5_), channel_id=1, source_target_pairs={{0,2},{1,31},{2,4},{3,1},{4,6},{5,3},{6,8},{7,5},{8,10},{9,7},{10,... | collective-permute-start | bytes 3145736 | tf_op jit(solution)/shard_map/ppermute | solution.py:102
  85.3 33.4 %all-to-all-start.2 = ((bf16[16,256,256]{2,1,0:T(8,128)(2,1)}), bf16[16,256,256]{2,1,0:T(8,128)(2,1)}, u32[]{:S(2)}, u32[]{:S(2)}) async-start(bf16[16,256,256]{2,1,0:T(8,128)(2,1)} %shard_map.47), calls=%async_computation.2 | async-start | bytes 4194304 | tf_op jit(solution)/shard_map/all_to_all | solution.py:145
  91.9 19.8 %collective-permute-start.9 = (bf16[512,1024]{1,0:T(8,128)(2,1)}, bf16[512,1024]{1,0:T(8,128)(2,1)S(1)}, u32[]{:S(2)}, u32[]{:S(2)}) collective-permute-start(bf16[512,1024]{1,0:T(8,128)(2,1)} %collective-permute-done.6.refs_0_), channel_id=1, source_target_pairs={{0,1},{1,0},{2,3},{3,2},{4,5},{5,4},{6,7},{7,6},{8,9},{9,8},{10,11... | collective-permute-start | bytes 3145736 | tf_op jit(solution)/shard_map/ppermute | solution.py:102
  107.9 17.9 %collective-permute-start.11 = (bf16[512,1024]{1,0:T(8,128)(2,1)}, bf16[512,1024]{1,0:T(8,128)(2,1)}, u32[]{:S(2)}, u32[]{:S(2)}) collective-permute-start(bf16[512,1024]{1,0:T(8,128)(2,1)} %collective-permute-done.6.refs_0_), channel_id=1, source_target_pairs={{0,2},{1,31},{2,4},{3,1},{4,6},{5,3},{6,8},{7,5},{8,10},{9,7},{10,... | collective-permute-start | bytes 3145736 | tf_op jit(solution)/shard_map/ppermute | solution.py:102
  109.8 25.5 %collective-permute-start.12 = (bf16[512,1024]{1,0:T(8,128)(2,1)}, bf16[512,1024]{1,0:T(8,128)(2,1)}, u32[]{:S(2)}, u32[]{:S(2)}) collective-permute-start(bf16[512,1024]{1,0:T(8,128)(2,1)} %collective-permute-done.7.refs_5_), channel_id=1, source_target_pairs={{0,2},{1,31},{2,4},{3,1},{4,6},{5,3},{6,8},{7,5},{8,10},{9,7},{10,... | collective-permute-start | bytes 3145736 | tf_op jit(solution)/shard_map/ppermute | solution.py:102
  118.7 34.4 %all-to-all-start.3 = ((bf16[16,256,256]{2,1,0:T(8,128)(2,1)}), bf16[16,256,256]{2,1,0:T(8,128)(2,1)}, u32[]{:S(2)}, u32[]{:S(2)}) async-start(bf16[16,256,256]{2,1,0:T(8,128)(2,1)} %shard_map.48), calls=%async_computation.3 | async-start | bytes 4194304 | tf_op jit(solution)/shard_map/all_to_all | solution.py:145
  125.8 17.3 %collective-permute-start.14 = (bf16[512,1024]{1,0:T(8,128)(2,1)}, bf16[512,1024]{1,0:T(8,128)(2,1)S(1)}, u32[]{:S(2)}, u32[]{:S(2)}) collective-permute-start(bf16[512,1024]{1,0:T(8,128)(2,1)} %collective-permute-done.11.refs_0_), channel_id=1, source_target_pairs={{0,1},{1,0},{2,3},{3,2},{4,5},{5,4},{6,7},{7,6},{8,9},{9,8},{10,11... | collective-permute-start | bytes 3145736 | tf_op jit(solution)/shard_map/ppermute | solution.py:102
  139.3 20.3 %collective-permute-start.16 = (bf16[512,1024]{1,0:T(8,128)(2,1)}, bf16[512,1024]{1,0:T(8,128)(2,1)}, u32[]{:S(2)}, u32[]{:S(2)}) collective-permute-start(bf16[512,1024]{1,0:T(8,128)(2,1)} %collective-permute-done.11.refs_0_), channel_id=1, source_target_pairs={{0,2},{1,31},{2,4},{3,1},{4,6},{5,3},{6,8},{7,5},{8,10},{9,7},{10,... | collective-permute-start | bytes 3145736 | tf_op jit(solution)/shard_map/ppermute | solution.py:102
  141.2 25.5 %collective-permute-start.17 = (bf16[512,1024]{1,0:T(8,128)(2,1)}, bf16[512,1024]{1,0:T(8,128)(2,1)}, u32[]{:S(2)}, u32[]{:S(2)}) collective-permute-start(bf16[512,1024]{1,0:T(8,128)(2,1)} %collective-permute-done.12.refs_5_), channel_id=1, source_target_pairs={{0,2},{1,31},{2,4},{3,1},{4,6},{5,3},{6,8},{7,5},{8,10},{9,7},{10,... | collective-permute-start | bytes 3145736 | tf_op jit(solution)/shard_map/ppermute | solution.py:102
  153.1 33.0 %all-to-all-start.4 = ((bf16[16,256,256]{2,1,0:T(8,128)(2,1)}), bf16[16,256,256]{2,1,0:T(8,128)(2,1)}, u32[]{:S(2)}, u32[]{:S(2)}) async-start(bf16[16,256,256]{2,1,0:T(8,128)(2,1)} %shard_map.49), calls=%async_computation.4 | async-start | bytes 4194304 | tf_op jit(solution)/shard_map/all_to_all | solution.py:145
  159.6 20.4 %collective-permute-start.19 = (bf16[512,1024]{1,0:T(8,128)(2,1)}, bf16[512,1024]{1,0:T(8,128)(2,1)S(1)}, u32[]{:S(2)}, u32[]{:S(2)}) collective-permute-start(bf16[512,1024]{1,0:T(8,128)(2,1)} %collective-permute-done.16.refs_0_), channel_id=1, source_target_pairs={{0,1},{1,0},{2,3},{3,2},{4,5},{5,4},{6,7},{7,6},{8,9},{9,8},{10,11... | collective-permute-start | bytes 3145736 | tf_op jit(solution)/shard_map/ppermute | solution.py:102
  175.7 64.5 %collective-permute-start.24 = (bf16[4,16,256]{2,1,0:T(8,128)(2,1)S(1)}, bf16[4,16,256]{2,1,0:T(8,128)(2,1)S(1)}, u32[]{:S(2)}, u32[]{:S(2)}) collective-permute-start(bf16[4,16,256]{2,1,0:T(8,128)(2,1)S(1)} %get-tuple-element.9), channel_id=1, source_target_pairs={{0,31},{1,2},{2,1},{3,4},{4,3},{5,6},{6,5},{7,8},{8,7},{9,10},{10,... | collective-permute-start | bytes 98312 | tf_op jit(solution)/shard_map/ppermute | solution.py:102
  186.0 30.1 %all-to-all-start.5 = ((bf16[16,192,256]{2,1,0:T(8,128)(2,1)}), bf16[16,192,256]{2,1,0:T(8,128)(2,1)S(1)}, u32[]{:S(2)}, u32[]{:S(2)}) async-start(bf16[16,192,256]{2,1,0:T(8,128)(2,1)} %shard_map.50), calls=%async_computation.5 | async-start | bytes 3145728 | tf_op jit(solution)/shard_map/all_to_all | solution.py:145
  195.2 15.1 %collective-permute-start.10 = (bf16[4,16,256]{2,1,0:T(8,128)(2,1)S(1)}, bf16[4,16,256]{2,1,0:T(8,128)(2,1)S(1)}, u32[]{:S(2)}, u32[]{:S(2)}) collective-permute-start(bf16[4,16,256]{2,1,0:T(8,128)(2,1)S(1)} %get-tuple-element.12), channel_id=1, source_target_pairs={{0,28},{1,5},{2,30},{3,7},{4,0},{5,9},{6,2},{7,11},{8,4},{9,13},{1... | collective-permute-start | bytes 98312 | tf_op jit(solution)/shard_map/ppermute | solution.py:102
  203.4 36.8 %collective-permute-start.23 = (bf16[4,16,256]{2,1,0:T(8,128)(2,1)S(1)}, bf16[4,16,256]{2,1,0:T(8,128)(2,1)S(1)}, u32[]{:S(2)}, u32[]{:S(2)}) collective-permute-start(bf16[4,16,256]{2,1,0:T(8,128)(2,1)S(1)} %get-tuple-element.11), channel_id=1, source_target_pairs={{0,29},{1,4},{2,31},{3,6},{4,1},{5,8},{6,3},{7,10},{8,5},{9,12},{1... | collective-permute-start | bytes 98312 | tf_op jit(solution)/shard_map/ppermute | solution.py:102
  210.3 29.8 %collective-permute-start.22 = (bf16[4,16,256]{2,1,0:T(8,128)(2,1)S(1)}, bf16[4,16,256]{2,1,0:T(8,128)(2,1)S(1)}, u32[]{:S(2)}, u32[]{:S(2)}) collective-permute-start(bf16[4,16,256]{2,1,0:T(8,128)(2,1)S(1)} %get-tuple-element.13), channel_id=1, source_target_pairs={{0,27},{1,6},{2,29},{3,8},{4,31},{5,10},{6,1},{7,12},{8,3},{9,14},... | collective-permute-start | bytes 98312 | tf_op jit(solution)/shard_map/ppermute | solution.py:102
  216.4 20.4 %collective-permute-start.20 = (bf16[4,16,256]{2,1,0:T(8,128)(2,1)S(1)}, bf16[4,16,256]{2,1,0:T(8,128)(2,1)S(1)}, u32[]{:S(2)}, u32[]{:S(2)}) collective-permute-start(bf16[4,16,256]{2,1,0:T(8,128)(2,1)S(1)} %slice_bitcast_fusion.11), channel_id=1, source_target_pairs={{0,24},{1,9},{2,26},{3,11},{4,28},{5,13},{6,30},{7,15},{8,0},{9,17... | collective-permute-start | bytes 98312 | tf_op jit(solution)/shard_map/ppermute | solution.py:102
  (14 other events, 111.7 us)

commit v3 on v2

--- a/solution.py
+++ b/solution.py
@@ -8,37 +8,42 @@
 from jax.sharding import Mesh
 from jax.sharding import PartitionSpec as P
 
+
 B = 256
 EPSILON = 1e-05
 RING = ("z", "core")
+INFO = 16
 
 
-def entry_at(cell, ring, place):
-    away, back, first_other, second_other = cell
-    chip, core = place[0], place[1]
-    sign = 1 - 2 * core
-    owner = lax.rem(chip - sign * back + ring, ring)
-    distance = lax.rem(sign * away + ring, ring)
-    first = 1 - core if first_other else core
-    second = 1 - core if second_other else core
-    return ((owner * 2 + first) * ring + distance) * 2 + second
+def column_of(cell, ring, place):
+    away, _, second_other = cell
+    core = place[1]
+    distance = lax.rem((1 - 2 * core) * away + ring, ring)
+    return distance * 2 + (1 - core if second_other else core)
 
 
-def tile_kernel(cells, where, ring, table, place, residual, *refs):
+def tile_kernel(cells, where, ring, place, residual, info_ref, *refs):
     out = refs[-1]
     parts = out.shape[0]
     depth = B // parts
-    for j, (cell, (a_at, c_at)) in enumerate(zip(cells, where)):
-        entry = table[entry_at(cell, ring, place)]
+    count = residual.shape[0]
+    entries = []
+    for cell in cells:
+        start = count + (0 if cell[1] else INFO)
+        line = info_ref[start : start + INFO, 0:128].astype(jnp.float32)
+        spot = lax.broadcasted_iota(jnp.int32, line.shape, 1) == column_of(cell, ring, place)
+        entries.append(jnp.sum(jnp.where(spot, line, 0.0)).astype(jnp.int32))
+    for j, (a_at, c_at) in enumerate(where):
+        entry = entries[j]
         rows = slice(2 * j * depth, 2 * (j + 1) * depth)
 
         @pl.when(entry > 0)
         def _(a_ref=refs[a_at], c_ref=refs[c_at], j=j, entry=entry):
             first = pl.multiple_of((entry - 1) // 4 * B, B)
             second = pl.multiple_of(lax.rem(entry - 1, 4) * B, B)
-            left = a_ref[:, pl.ds(first, B)].astype(jnp.float32)
+            left = a_ref[0:count, pl.ds(first, B)].astype(jnp.float32)
             weighted = (residual[...] * left).astype(jnp.bfloat16)
-            right = c_ref[:, pl.ds(second, B)]
+            right = c_ref[0:count, pl.ds(second, B)]
             over_rows = (((0,), (0,)), ((), ()))
             cross = lax.dot_general(
                 weighted, right, over_rows, preferred_element_type=jnp.float32
@@ -56,7 +61,7 @@
             out[:, rows, :] = jnp.zeros((parts, 2 * depth, B), jnp.bfloat16)
 
 
-def tiles(cells, operands, ring, parts, table, place, residual):
+def tiles(cells, operands, info, ring, parts, place, residual):
     arrays, where = [], []
     for pair in operands:
         spots = []
@@ -73,7 +78,7 @@
     return pl.pallas_call(
         functools.partial(tile_kernel, cells, where, ring),
         out_shape=jax.ShapeDtypeStruct(shape, jnp.bfloat16),
-        in_specs=[smem, smem, vmem] + [vmem] * len(arrays),
+        in_specs=[smem, vmem, vmem] + [vmem] * len(arrays),
         out_specs=vmem,
         cost_estimate=pl.CostEstimate(
             flops=len(cells) * 4 * rows * B * B,
@@ -81,10 +86,10 @@
             transcendentals=0,
         ),
         compiler_params=pltpu.CompilerParams(vmem_limit_bytes=24 << 20),
-    )(table, place, residual, *arrays)
+    )(place, residual, info, *arrays)
 
 
-def on_device(dosage, residual, pairs, counts):
+def scores_of(dosage, residual, pairs, counts):
     ring = lax.axis_size("z")
     parts = lax.axis_size("ind")
     chip, core = lax.axis_index("z"), lax.axis_index("core")
@@ -113,19 +118,19 @@
     wanted = (position[:, None] == jnp.arange(2 * ring, dtype=jnp.int32)[None, :]) & live[:, None]
     code = 1 + first_local * local_blocks + second_local
     row = jnp.sum(jnp.where(wanted, code[:, None], 0), axis=0)
-    rows = jnp.broadcast_to(row[None, :], (2 * ring, 2 * ring))
-    table = lax.all_to_all(rows, RING, 0, 0, tiled=True).reshape(-1)
+    info = jnp.pad(row.astype(jnp.bfloat16)[None, :], ((0, INFO - 1), (0, dosage.shape[1] - 2 * ring)))
     place = jnp.stack([chip, core]).astype(jnp.int32)
     column = residual[:, None]
 
     hops = ring // 4
-    own, other = [dosage], [swap(dosage)]
+    across = swap(jnp.concatenate([dosage, info]))
+    own, other = [dosage], [jnp.concatenate([across, info])]
     far_own, far_other = [dosage], [other[0]]
     near, cross = {}, {}
     for h in range(0, hops + 1):
         cells, operands = [], []
         if h == 0:
-            cells = [(0, 0, False, False), (0, 0, False, True)]
+            cells = [(0, False, False), (0, False, True)]
             operands = [(dosage, dosage), (dosage, other[0])]
         else:
             own.append(move(own[h - 1], 1))
@@ -139,9 +144,9 @@
                         continue
                     for second_other in (False, True):
                         c = far_other[at] if second_other else far_own[at]
-                        cells.append((away_by, h, first_other, second_other))
+                        cells.append((away_by, first_other, second_other))
                         operands.append((a, c))
-        partial = tiles(tuple(cells), operands, ring, parts, table, place, column)
+        partial = tiles(tuple(cells), operands, other[h], ring, parts, place, column)
         arrived = lax.all_to_all(partial, "ind", 0, 0, tiled=True)
         summed = jnp.sum(arrived.astype(jnp.float32), axis=0)
         summed = summed.reshape(len(cells), 2, depth, B)
@@ -169,6 +174,4 @@
     devices = mesh.devices.reshape(mesh.shape["ind"], mesh.shape["blk"] // 2, 2)
     torus = Mesh(devices, ("ind", *RING))
     placed = (P("ind", RING), P("ind"), P(RING, None), P(RING))
-    return jax.shard_map(
-        on_device, mesh=torus, in_specs=placed, out_specs=P("ind", RING, None), check_vma=False
-    )
+    return jax.shard_map(scores_of, mesh=torus, in_specs=placed, out_specs=P("ind", RING, None), check_vma=False)

time: 241 us -> 230 us (0.954); the launches traced: 242 us -> 227 us
  starting transfers between devices: 148 us -> 120 us
  waiting for transfers between devices: 55.4 us -> 61.7 us
  local copies, waits for them, and re-layouts: 8.58 us -> 12.1 us
  other arithmetic: 9.63 us -> 12.2 us
    all_to_all x6 -> x5, starting transfers between devices: 43.4 us -> 26 us  [scores_of(): arrived = lax.all_to_all(partial, 'ind', 0, 0, tiled=True)]
    all_to_all x6 -> x5, waiting for transfers between devices: 16.9 us -> 32.4 us  [scores_of(): arrived = lax.all_to_all(partial, 'ind', 0, 0, tiled=True)]
    ppermute x25, starting transfers between devices: 104 us -> 94.3 us  [move(): return lax.ppermute(x, RING, perm)]
    ppermute x25, waiting for transfers between devices: 38.5 us -> 29.3 us  [move(): return lax.ppermute(x, RING, perm)]
    unnamed x24 -> x30, local copies, waits for them, and re-layouts: 5.27 us -> 9.34 us
  transfers between devices with their start and end apart: 31 -> 30, of which waited for: 11 -> 10; matrix products, arithmetic and copies ran while one was open for 5% -> 4% of each run, Pallas kernels for 8% -> 8%
where the time goes in v3:
time: 230 us; the launch traced here: 227 us
  starting transfers between devices  120 us (52%)
  waiting for transfers between devices  61.7 us (27%)
  Pallas kernels  19.1 us (8%)
  other arithmetic  12.2 us (5%)
  local copies, waits for them, and re-layouts  12.1 us (5%)
    ppermute x25, starting transfers between devices, move(): return lax.ppermute(x, RING, perm)  94.3 us
    all_to_all x5, waiting for transfers between devices, scores_of(): arrived = lax.all_to_all(partial, 'ind', 0, 0, tiled=True)  32.4 us
    ppermute x25, waiting for transfers between devices, move(): return lax.ppermute(x, RING, perm)  29.3 us
    all_to_all x5, starting transfers between devices, scores_of(): arrived = lax.all_to_all(partial, 'ind', 0, 0, tiled=True)  26 us
    pallas_call x5, Pallas kernels, tiles(): pl.pallas_call(functools.partial(tile_kernel, cells, where, ring), out_sh...  19.1 us
    unnamed x30, local copies, waits for them, and re-layouts  9.34 us
    reduce_sum x5, other arithmetic, scores_of(): summed = jnp.sum(arrived.astype(jnp.float32), axis=0)  7.05 us
  transfers between devices with their start and end apart: 30, of which 10 were waited for; matrix products, arithmetic and copies ran while one was open for 4% of the time, Pallas kernels for 8%

profile of v3, /device:TPU:1, one launch (start us, length us, event | category | flops | bytes accessed | tf_op | source)
XLA Modules:
  0.0 226.7 jit_solution(1821148951163125439)
XLA Ops:
  4.2 8.9 %collective-permute-start = (bf16[528,1024]{1,0:T(8,128)(2,1)S(1)}, bf16[528,1024]{1,0:T(8,128)(2,1)S(1)}, u32[]{:S(2)}, u32[]{:S(2)}) collective-permute-start(bf16[528,1024]{1,0:T(8,128)(2,1)S(1)} %pad_maximum_fusion.1), channel_id=1, source_target_pairs={{0,1},{1,0},{2,3},{3,2},{4,5},{5,4},{6,7},{7,6},{8,9},{9,8},{10,11... | collective-permute-start | bytes 3244040 | tf_op jit(solution)/shard_map/ppermute | solution.py:107
  15.5 5.8 %collective-permute-start.1 = (bf16[544,1024]{1,0:T(8,128)(2,1)S(1)}, bf16[544,1024]{1,0:T(8,128)(2,1)}, u32[]{:S(2)}, u32[]{:S(2)}) collective-permute-start(bf16[544,1024]{1,0:T(8,128)(2,1)S(1)} %pad_maximum_fusion.info_ref.refs_1_.refs_2_), channel_id=1, source_target_pairs={{0,2},{1,31},{2,4},{3,1},{4,6},{5,3},{6,8},{7,5},{8,10},{9,7},{10,... | collective-permute-start | bytes 3342344 | tf_op jit(solution)/shard_map/ppermute | solution.py:107
  23.9 9.8 %collective-permute-done.1.info_ref.refs_5_ = bf16[544,1024]{1,0:T(8,128)(2,1)} collective-permute-done((bf16[544,1024]{1,0:T(8,128)(2,1)S(1)}, bf16[544,1024]{1,0:T(8,128)(2,1)}, u32[]{:S(2)}, u32[]{:S(2)}) %collective-permute-start.1) | collective-permute-done | bytes 1114144 | tf_op jit(solution)/shard_map/ppermute | solution.py:107
  33.7 3.7 %collective-permute-start.3 = (bf16[544,1024]{1,0:T(8,128)(2,1)}, bf16[544,1024]{1,0:T(8,128)(2,1)S(1)}, u32[]{:S(2)}, u32[]{:S(2)}) collective-permute-start(bf16[544,1024]{1,0:T(8,128)(2,1)} %collective-permute-done.1.info_ref.refs_5_), channel_id=1, source_target_pairs={{0,1},{1,0},{2,3},{3,2},{4,5},{5,4},{6,7},{7,6},{8,9},{9,8},{10,11... | collective-permute-start | bytes 3342344 | tf_op jit(solution)/shard_map/ppermute | solution.py:107
  37.4 7.5 %collective-permute-done.2.refs_0_ = bf16[512,1024]{1,0:T(8,128)(2,1)} collective-permute-done((bf16[512,1024]{1,0:T(8,128)(2,1)S(1)}, bf16[512,1024]{1,0:T(8,128)(2,1)}, u32[]{:S(2)}, u32[]{:S(2)}) %collective-permute-start.2) | collective-permute-done | bytes 1048608 | tf_op jit(solution)/shard_map/ppermute | solution.py:107
  44.9 3.7 %collective-permute-start.4 = (bf16[512,1024]{1,0:T(8,128)(2,1)}, bf16[512,1024]{1,0:T(8,128)(2,1)}, u32[]{:S(2)}, u32[]{:S(2)}) collective-permute-start(bf16[512,1024]{1,0:T(8,128)(2,1)} %collective-permute-done.2.refs_0_), channel_id=1, source_target_pairs={{0,1},{1,0},{2,3},{3,2},{4,5},{5,4},{6,7},{7,6},{8,9},{9,8},{10,11... | collective-permute-start | bytes 3145736 | tf_op jit(solution)/shard_map/ppermute | solution.py:107
  50.8 6.8 %all-to-all-start = ((bf16[16,64,256]{2,1,0:T(8,128)(2,1)}), bf16[16,64,256]{2,1,0:T(8,128)(2,1)}, u32[]{:S(2)}, u32[]{:S(2)}) async-start(bf16[16,64,256]{2,1,0:T(8,128)(2,1)} %copy-done.6), calls=%async_computation | async-start | bytes 1048576 | tf_op jit(solution)/shard_map/all_to_all | solution.py:150
  63.5 4.4 %shard_map.47 = bf16[16,256,256]{2,1,0:T(8,128)(2,1)S(1)} custom-call(s32[2]{0:T(128)S(1)} %pad_add_fusion.place, f32[512,1]{1,0:T(8,128)S(1)} %copy.34.residual, bf16[544,1024]{1,0:T(8,128)(2,1)} %collective-permute-done.1.info_ref.refs_5_, bf16[512,1024]{1,0:T(8,128)(2,1)} %collective-permute-done.2.refs_0_, bf16[512,1024]{1,0:T(8,128)(2,1)S(1)} %copy-done, ...), custom_call_target="tpu_custom_call" | custom-call | flops 1073741824 | bytes 6291456 | tf_op jit(solution)/shard_map/pallas_call | solution.py:78
  69.3 6.6 %all-to-all-start.1 = ((bf16[16,256,256]{2,1,0:T(8,128)(2,1)}), bf16[16,256,256]{2,1,0:T(8,128)(2,1)S(1)}, u32[]{:S(2)}, u32[]{:S(2)}) async-start(bf16[16,256,256]{2,1,0:T(8,128)(2,1)} %copy-done.1), calls=%async_computation.1 | async-start | bytes 4194304 | tf_op jit(solution)/shard_map/all_to_all | solution.py:150
  78.8 7.0 %collective-permute-done.7.refs_0_ = bf16[512,1024]{1,0:T(8,128)(2,1)} collective-permute-done((bf16[512,1024]{1,0:T(8,128)(2,1)}, bf16[512,1024]{1,0:T(8,128)(2,1)}, u32[]{:S(2)}, u32[]{:S(2)}) %collective-permute-start.7) | collective-permute-done | bytes 1048608 | tf_op jit(solution)/shard_map/ppermute | solution.py:107
  85.7 4.3 %collective-permute-start.9 = (bf16[512,1024]{1,0:T(8,128)(2,1)}, bf16[512,1024]{1,0:T(8,128)(2,1)S(1)}, u32[]{:S(2)}, u32[]{:S(2)}) collective-permute-start(bf16[512,1024]{1,0:T(8,128)(2,1)} %collective-permute-done.7.refs_0_), channel_id=1, source_target_pairs={{0,1},{1,0},{2,3},{3,2},{4,5},{5,4},{6,7},{7,6},{8,9},{9,8},{10,11... | collective-permute-start | bytes 3145736 | tf_op jit(solution)/shard_map/ppermute | solution.py:107
  95.1 5.7 %shard_map.48 = bf16[16,256,256]{2,1,0:T(8,128)(2,1)} custom-call(s32[2]{0:T(128)S(1)} %pad_add_fusion.place, f32[512,1]{1,0:T(8,128)S(1)} %copy.34.residual, bf16[544,1024]{1,0:T(8,128)(2,1)} %collective-permute-done.6.info_ref.refs_5_, bf16[512,1024]{1,0:T(8,128)(2,1)} %collective-permute-done.7.refs_0_, ...), custom_call_target="tpu_custom_call" | custom-call | flops 1073741824 | bytes 6291456 | tf_op jit(solution)/shard_map/pallas_call | solution.py:78
  102.8 6.3 %all-to-all-done.1 = bf16[16,256,256]{2,1,0:T(8,128)(2,1)S(1)} async-done(((bf16[16,256,256]{2,1,0:T(8,128)(2,1)}), bf16[16,256,256]{2,1,0:T(8,128)(2,1)S(1)}, u32[]{:S(2)}, u32[]{:S(2)}) %all-to-all-start.1) | async-done | bytes 2097184 | tf_op jit(solution)/shard_map/all_to_all | solution.py:150
  110.4 4.4 %all-to-all-start.2 = ((bf16[16,256,256]{2,1,0:T(8,128)(2,1)}), bf16[16,256,256]{2,1,0:T(8,128)(2,1)}, u32[]{:S(2)}, u32[]{:S(2)}) async-start(bf16[16,256,256]{2,1,0:T(8,128)(2,1)} %shard_map.48), calls=%async_computation.2 | async-start | bytes 4194304 | tf_op jit(solution)/shard_map/all_to_all | solution.py:150
  118.1 4.0 %collective-permute-start.14 = (bf16[512,1024]{1,0:T(8,128)(2,1)}, bf16[512,1024]{1,0:T(8,128)(2,1)S(1)}, u32[]{:S(2)}, u32[]{:S(2)}) collective-permute-start(bf16[512,1024]{1,0:T(8,128)(2,1)} %collective-permute-done.12.refs_0_), channel_id=1, source_target_pairs={{0,1},{1,0},{2,3},{3,2},{4,5},{5,4},{6,7},{7,6},{8,9},{9,8},{10,11... | collective-permute-start | bytes 3145736 | tf_op jit(solution)/shard_map/ppermute | solution.py:107
  129.8 4.8 %shard_map.49 = bf16[16,256,256]{2,1,0:T(8,128)(2,1)} custom-call(s32[2]{0:T(128)S(1)} %pad_add_fusion.place, f32[512,1]{1,0:T(8,128)S(1)} %copy.34.residual, bf16[544,1024]{1,0:T(8,128)(2,1)} %collective-permute-done.11.info_ref.refs_5_, bf16[512,1024]{1,0:T(8,128)(2,1)} %collective-permute-done.12.refs_0_, bf16[544,1024]{1,0:T(8,128)(2,1)S(1)} %copy-done.3, ...), custom_call_target="tpu_custom_call" | custom-call | flops 1073741824 | bytes 6291456 | tf_op jit(solution)/shard_map/pallas_call | solution.py:78
  134.6 14.0 %all-to-all-done.2 = bf16[16,256,256]{2,1,0:T(8,128)(2,1)} async-done(((bf16[16,256,256]{2,1,0:T(8,128)(2,1)}), bf16[16,256,256]{2,1,0:T(8,128)(2,1)}, u32[]{:S(2)}, u32[]{:S(2)}) %all-to-all-start.2) | async-done | bytes 2097184 | tf_op jit(solution)/shard_map/all_to_all | solution.py:150
  148.6 4.4 %all-to-all-start.3 = ((bf16[16,256,256]{2,1,0:T(8,128)(2,1)}), bf16[16,256,256]{2,1,0:T(8,128)(2,1)}, u32[]{:S(2)}, u32[]{:S(2)}) async-start(bf16[16,256,256]{2,1,0:T(8,128)(2,1)} %shard_map.49), calls=%async_computation.3 | async-start | bytes 4194304 | tf_op jit(solution)/shard_map/all_to_all | solution.py:150
  164.7 4.0 %collective-permute-start.24 = (bf16[4,16,256]{2,1,0:T(8,128)(2,1)}, bf16[4,16,256]{2,1,0:T(8,128)(2,1)}, u32[]{:S(2)}, u32[]{:S(2)}) collective-permute-start(bf16[4,16,256]{2,1,0:T(8,128)(2,1)} %get-tuple-element.9), channel_id=1, source_target_pairs={{0,31},{1,2},{2,1},{3,4},{4,3},{5,6},{6,5},{7,8},{8,7},{9,10},{10,... | collective-permute-start | bytes 98312 | tf_op jit(solution)/shard_map/ppermute | solution.py:107
  172.4 11.8 %all-to-all-done.3 = bf16[16,256,256]{2,1,0:T(8,128)(2,1)} async-done(((bf16[16,256,256]{2,1,0:T(8,128)(2,1)}), bf16[16,256,256]{2,1,0:T(8,128)(2,1)}, u32[]{:S(2)}, u32[]{:S(2)}) %all-to-all-start.3) | async-done | bytes 2097184 | tf_op jit(solution)/shard_map/all_to_all | solution.py:150
  184.3 3.7 %all-to-all-start.4 = ((bf16[16,192,256]{2,1,0:T(8,128)(2,1)}), bf16[16,192,256]{2,1,0:T(8,128)(2,1)S(1)}, u32[]{:S(2)}, u32[]{:S(2)}) async-start(bf16[16,192,256]{2,1,0:T(8,128)(2,1)} %shard_map.50), calls=%async_computation.4 | async-start | bytes 3145728 | tf_op jit(solution)/shard_map/all_to_all | solution.py:150
  192.9 5.2 %collective-permute-start.23 = (bf16[4,16,256]{2,1,0:T(8,128)(2,1)S(1)}, bf16[4,16,256]{2,1,0:T(8,128)(2,1)S(1)}, u32[]{:S(2)}, u32[]{:S(2)}) collective-permute-start(bf16[4,16,256]{2,1,0:T(8,128)(2,1)S(1)} %get-tuple-element.11), channel_id=1, source_target_pairs={{0,29},{1,4},{2,31},{3,6},{4,1},{5,8},{6,3},{7,10},{8,5},{9,12},{1... | collective-permute-start | bytes 98312 | tf_op jit(solution)/shard_map/ppermute | solution.py:107
  202.0 6.5 %collective-permute-start.22 = (bf16[4,16,256]{2,1,0:T(8,128)(2,1)S(1)}, bf16[4,16,256]{2,1,0:T(8,128)(2,1)S(1)}, u32[]{:S(2)}, u32[]{:S(2)}) collective-permute-start(bf16[4,16,256]{2,1,0:T(8,128)(2,1)S(1)} %get-tuple-element.13), channel_id=1, source_target_pairs={{0,27},{1,6},{2,29},{3,8},{4,31},{5,10},{6,1},{7,12},{8,3},{9,14},... | collective-permute-start | bytes 98312 | tf_op jit(solution)/shard_map/ppermute | solution.py:107
  211.4 11.0 %collective-permute-start.21 = (bf16[2,16,256]{2,1,0:T(8,128)(2,1)S(1)}, bf16[2,16,256]{2,1,0:T(8,128)(2,1)S(1)}, u32[]{:S(2)}, u32[]{:S(2)}) collective-permute-start(bf16[2,16,256]{2,1,0:T(8,128)(2,1)S(1)} %slice_bitcast_fusion.17), channel_id=1, source_target_pairs={{0,25},{1,8},{2,27},{3,10},{4,29},{5,12},{6,31},{7,14},{8,1},{9,16... | collective-permute-start | bytes 49160 | tf_op jit(solution)/shard_map/ppermute | solution.py:107
  (101 shorter events, 71.2 us)
Async XLA Ops:
  15.5 18.2 %collective-permute-start.1 = (bf16[544,1024]{1,0:T(8,128)(2,1)S(1)}, bf16[544,1024]{1,0:T(8,128)(2,1)}, u32[]{:S(2)}, u32[]{:S(2)}) collective-permute-start(bf16[544,1024]{1,0:T(8,128)(2,1)S(1)} %pad_maximum_fusion.info_ref.refs_1_.refs_2_), channel_id=1, source_target_pairs={{0,2},{1,31},{2,4},{3,1},{4,6},{5,3},{6,8},{7,5},{8,10},{9,7},{10,... | collective-permute-start | bytes 3342344 | tf_op jit(solution)/shard_map/ppermute | solution.py:107
  21.3 23.6 %collective-permute-start.2 = (bf16[512,1024]{1,0:T(8,128)(2,1)S(1)}, bf16[512,1024]{1,0:T(8,128)(2,1)}, u32[]{:S(2)}, u32[]{:S(2)}) collective-permute-start(bf16[512,1024]{1,0:T(8,128)(2,1)S(1)} %copy-done), channel_id=1, source_target_pairs={{0,2},{1,31},{2,4},{3,1},{4,6},{5,3},{6,8},{7,5},{8,10},{9,7},{10,... | collective-permute-start | bytes 3145736 | tf_op jit(solution)/shard_map/ppermute | solution.py:107
  33.7 29.8 %collective-permute-start.3 = (bf16[544,1024]{1,0:T(8,128)(2,1)}, bf16[544,1024]{1,0:T(8,128)(2,1)S(1)}, u32[]{:S(2)}, u32[]{:S(2)}) collective-permute-start(bf16[544,1024]{1,0:T(8,128)(2,1)} %collective-permute-done.1.info_ref.refs_5_), channel_id=1, source_target_pairs={{0,1},{1,0},{2,3},{3,2},{4,5},{5,4},{6,7},{7,6},{8,9},{9,8},{10,11... | collective-permute-start | bytes 3342344 | tf_op jit(solution)/shard_map/ppermute | solution.py:107
  44.9 18.6 %collective-permute-start.4 = (bf16[512,1024]{1,0:T(8,128)(2,1)}, bf16[512,1024]{1,0:T(8,128)(2,1)}, u32[]{:S(2)}, u32[]{:S(2)}) collective-permute-start(bf16[512,1024]{1,0:T(8,128)(2,1)} %collective-permute-done.2.refs_0_), channel_id=1, source_target_pairs={{0,1},{1,0},{2,3},{3,2},{4,5},{5,4},{6,7},{7,6},{8,9},{9,8},{10,11... | collective-permute-start | bytes 3145736 | tf_op jit(solution)/shard_map/ppermute | solution.py:107
  50.8 18.4 %all-to-all-start = ((bf16[16,64,256]{2,1,0:T(8,128)(2,1)}), bf16[16,64,256]{2,1,0:T(8,128)(2,1)}, u32[]{:S(2)}, u32[]{:S(2)}) async-start(bf16[16,64,256]{2,1,0:T(8,128)(2,1)} %copy-done.6), calls=%async_computation | async-start | bytes 1048576 | tf_op jit(solution)/shard_map/all_to_all | solution.py:150
  57.7 18.2 %collective-permute-start.6 = (bf16[544,1024]{1,0:T(8,128)(2,1)}, bf16[544,1024]{1,0:T(8,128)(2,1)}, u32[]{:S(2)}, u32[]{:S(2)}) collective-permute-start(bf16[544,1024]{1,0:T(8,128)(2,1)} %collective-permute-done.1.info_ref.refs_5_), channel_id=1, source_target_pairs={{0,2},{1,31},{2,4},{3,1},{4,6},{5,3},{6,8},{7,5},{8,10},{9,7},{10,... | collective-permute-start | bytes 3342344 | tf_op jit(solution)/shard_map/ppermute | solution.py:107
  60.9 24.9 %collective-permute-start.7 = (bf16[512,1024]{1,0:T(8,128)(2,1)}, bf16[512,1024]{1,0:T(8,128)(2,1)}, u32[]{:S(2)}, u32[]{:S(2)}) collective-permute-start(bf16[512,1024]{1,0:T(8,128)(2,1)} %collective-permute-done.2.refs_0_), channel_id=1, source_target_pairs={{0,2},{1,31},{2,4},{3,1},{4,6},{5,3},{6,8},{7,5},{8,10},{9,7},{10,... | collective-permute-start | bytes 3145736 | tf_op jit(solution)/shard_map/ppermute | solution.py:107
  69.3 39.8 %all-to-all-start.1 = ((bf16[16,256,256]{2,1,0:T(8,128)(2,1)}), bf16[16,256,256]{2,1,0:T(8,128)(2,1)S(1)}, u32[]{:S(2)}, u32[]{:S(2)}) async-start(bf16[16,256,256]{2,1,0:T(8,128)(2,1)} %copy-done.1), calls=%async_computation.1 | async-start | bytes 4194304 | tf_op jit(solution)/shard_map/all_to_all | solution.py:150
  75.9 19.2 %collective-permute-start.8 = (bf16[544,1024]{1,0:T(8,128)(2,1)}, bf16[544,1024]{1,0:T(8,128)(2,1)S(1)}, u32[]{:S(2)}, u32[]{:S(2)}) collective-permute-start(bf16[544,1024]{1,0:T(8,128)(2,1)} %collective-permute-done.6.info_ref.refs_5_), channel_id=1, source_target_pairs={{0,1},{1,0},{2,3},{3,2},{4,5},{5,4},{6,7},{7,6},{8,9},{9,8},{10,11... | collective-permute-start | bytes 3342344 | tf_op jit(solution)/shard_map/ppermute | solution.py:107
  90.0 24.9 %collective-permute-start.11 = (bf16[544,1024]{1,0:T(8,128)(2,1)}, bf16[544,1024]{1,0:T(8,128)(2,1)}, u32[]{:S(2)}, u32[]{:S(2)}) collective-permute-start(bf16[544,1024]{1,0:T(8,128)(2,1)} %collective-permute-done.6.info_ref.refs_5_), channel_id=1, source_target_pairs={{0,2},{1,31},{2,4},{3,1},{4,6},{5,3},{6,8},{7,5},{8,10},{9,7},{10,... | collective-permute-start | bytes 3342344 | tf_op jit(solution)/shard_map/ppermute | solution.py:107
  92.6 25.5 %collective-permute-start.12 = (bf16[512,1024]{1,0:T(8,128)(2,1)}, bf16[512,1024]{1,0:T(8,128)(2,1)}, u32[]{:S(2)}, u32[]{:S(2)}) collective-permute-start(bf16[512,1024]{1,0:T(8,128)(2,1)} %collective-permute-done.7.refs_0_), channel_id=1, source_target_pairs={{0,2},{1,31},{2,4},{3,1},{4,6},{5,3},{6,8},{7,5},{8,10},{9,7},{10,... | collective-permute-start | bytes 3145736 | tf_op jit(solution)/shard_map/ppermute | solution.py:107
  110.4 38.2 %all-to-all-start.2 = ((bf16[16,256,256]{2,1,0:T(8,128)(2,1)}), bf16[16,256,256]{2,1,0:T(8,128)(2,1)}, u32[]{:S(2)}, u32[]{:S(2)}) async-start(bf16[16,256,256]{2,1,0:T(8,128)(2,1)} %shard_map.48), calls=%async_computation.2 | async-start | bytes 4194304 | tf_op jit(solution)/shard_map/all_to_all | solution.py:150
  114.9 12.5 %collective-permute-start.13 = (bf16[544,1024]{1,0:T(8,128)(2,1)}, bf16[544,1024]{1,0:T(8,128)(2,1)S(1)}, u32[]{:S(2)}, u32[]{:S(2)}) collective-permute-start(bf16[544,1024]{1,0:T(8,128)(2,1)} %collective-permute-done.11.info_ref.refs_5_), channel_id=1, source_target_pairs={{0,1},{1,0},{2,3},{3,2},{4,5},{5,4},{6,7},{7,6},{8,9},{9,8},{10,11... | collective-permute-start | bytes 3342344 | tf_op jit(solution)/shard_map/ppermute | solution.py:107
  122.1 34.4 %collective-permute-start.16 = (bf16[544,1024]{1,0:T(8,128)(2,1)}, bf16[544,1024]{1,0:T(8,128)(2,1)S(1)}, u32[]{:S(2)}, u32[]{:S(2)}) collective-permute-start(bf16[544,1024]{1,0:T(8,128)(2,1)} %collective-permute-done.11.info_ref.refs_5_), channel_id=1, source_target_pairs={{0,2},{1,31},{2,4},{3,1},{4,6},{5,3},{6,8},{7,5},{8,10},{9,7},{10,... | collective-permute-start | bytes 3342344 | tf_op jit(solution)/shard_map/ppermute | solution.py:107
  124.0 29.7 %collective-permute-start.17 = (bf16[512,1024]{1,0:T(8,128)(2,1)}, bf16[512,1024]{1,0:T(8,128)(2,1)}, u32[]{:S(2)}, u32[]{:S(2)}) collective-permute-start(bf16[512,1024]{1,0:T(8,128)(2,1)} %collective-permute-done.12.refs_0_), channel_id=1, source_target_pairs={{0,2},{1,31},{2,4},{3,1},{4,6},{5,3},{6,8},{7,5},{8,10},{9,7},{10,... | collective-permute-start | bytes 3145736 | tf_op jit(solution)/shard_map/ppermute | solution.py:107
  148.6 35.7 %all-to-all-start.3 = ((bf16[16,256,256]{2,1,0:T(8,128)(2,1)}), bf16[16,256,256]{2,1,0:T(8,128)(2,1)}, u32[]{:S(2)}, u32[]{:S(2)}) async-start(bf16[16,256,256]{2,1,0:T(8,128)(2,1)} %shard_map.49), calls=%async_computation.3 | async-start | bytes 4194304 | tf_op jit(solution)/shard_map/all_to_all | solution.py:150
  153.7 15.6 %collective-permute-start.19 = (bf16[512,1024]{1,0:T(8,128)(2,1)}, bf16[512,1024]{1,0:T(8,128)(2,1)S(1)}, u32[]{:S(2)}, u32[]{:S(2)}) collective-permute-start(bf16[512,1024]{1,0:T(8,128)(2,1)} %collective-permute-done.17.refs_0_), channel_id=1, source_target_pairs={{0,1},{1,0},{2,3},{3,2},{4,5},{5,4},{6,7},{7,6},{8,9},{9,8},{10,11... | collective-permute-start | bytes 3145736 | tf_op jit(solution)/shard_map/ppermute | solution.py:107
  156.5 12.8 %collective-permute-start.18 = (bf16[544,1024]{1,0:T(8,128)(2,1)S(1)}, bf16[544,1024]{1,0:T(8,128)(2,1)S(1)}, u32[]{:S(2)}, u32[]{:S(2)}) collective-permute-start(bf16[544,1024]{1,0:T(8,128)(2,1)S(1)} %collective-permute-done.16.info_ref.refs_5_), channel_id=1, source_target_pairs={{0,1},{1,0},{2,3},{3,2},{4,5},{5,4},{6,7},{7,6},{8,9},{9,8},{10,11... | collective-permute-start | bytes 3342344 | tf_op jit(solution)/shard_map/ppermute | solution.py:107
  164.7 59.2 %collective-permute-start.24 = (bf16[4,16,256]{2,1,0:T(8,128)(2,1)}, bf16[4,16,256]{2,1,0:T(8,128)(2,1)}, u32[]{:S(2)}, u32[]{:S(2)}) collective-permute-start(bf16[4,16,256]{2,1,0:T(8,128)(2,1)} %get-tuple-element.9), channel_id=1, source_target_pairs={{0,31},{1,2},{2,1},{3,4},{4,3},{5,6},{6,5},{7,8},{8,7},{9,10},{10,... | collective-permute-start | bytes 98312 | tf_op jit(solution)/shard_map/ppermute | solution.py:107
  184.3 24.6 %all-to-all-start.4 = ((bf16[16,192,256]{2,1,0:T(8,128)(2,1)}), bf16[16,192,256]{2,1,0:T(8,128)(2,1)S(1)}, u32[]{:S(2)}, u32[]{:S(2)}) async-start(bf16[16,192,256]{2,1,0:T(8,128)(2,1)} %shard_map.50), calls=%async_computation.4 | async-start | bytes 3145728 | tf_op jit(solution)/shard_map/all_to_all | solution.py:150
  192.9 31.0 %collective-permute-start.23 = (bf16[4,16,256]{2,1,0:T(8,128)(2,1)S(1)}, bf16[4,16,256]{2,1,0:T(8,128)(2,1)S(1)}, u32[]{:S(2)}, u32[]{:S(2)}) collective-permute-start(bf16[4,16,256]{2,1,0:T(8,128)(2,1)S(1)} %get-tuple-element.11), channel_id=1, source_target_pairs={{0,29},{1,4},{2,31},{3,6},{4,1},{5,8},{6,3},{7,10},{8,5},{9,12},{1... | collective-permute-start | bytes 98312 | tf_op jit(solution)/shard_map/ppermute | solution.py:107
  202.0 21.8 %collective-permute-start.22 = (bf16[4,16,256]{2,1,0:T(8,128)(2,1)S(1)}, bf16[4,16,256]{2,1,0:T(8,128)(2,1)S(1)}, u32[]{:S(2)}, u32[]{:S(2)}) collective-permute-start(bf16[4,16,256]{2,1,0:T(8,128)(2,1)S(1)} %get-tuple-element.13), channel_id=1, source_target_pairs={{0,27},{1,6},{2,29},{3,8},{4,31},{5,10},{6,1},{7,12},{8,3},{9,14},... | collective-permute-start | bytes 98312 | tf_op jit(solution)/shard_map/ppermute | solution.py:107
  209.1 13.3 %collective-permute-start.20 = (bf16[4,16,256]{2,1,0:T(8,128)(2,1)S(1)}, bf16[4,16,256]{2,1,0:T(8,128)(2,1)S(1)}, u32[]{:S(2)}, u32[]{:S(2)}) collective-permute-start(bf16[4,16,256]{2,1,0:T(8,128)(2,1)S(1)} %slice_bitcast_fusion.11), channel_id=1, source_target_pairs={{0,24},{1,9},{2,26},{3,11},{4,28},{5,13},{6,30},{7,15},{8,0},{9,17... | collective-permute-start | bytes 98312 | tf_op jit(solution)/shard_map/ppermute | solution.py:107
  211.4 12.4 %collective-permute-start.21 = (bf16[2,16,256]{2,1,0:T(8,128)(2,1)S(1)}, bf16[2,16,256]{2,1,0:T(8,128)(2,1)S(1)}, u32[]{:S(2)}, u32[]{:S(2)}) collective-permute-start(bf16[2,16,256]{2,1,0:T(8,128)(2,1)S(1)} %slice_bitcast_fusion.17), channel_id=1, source_target_pairs={{0,25},{1,8},{2,27},{3,10},{4,29},{5,12},{6,31},{7,14},{8,1},{9,16... | collective-permute-start | bytes 49160 | tf_op jit(solution)/shard_map/ppermute | solution.py:107
  (16 other events, 138.6 us)

commit v4 on v3

v4 whole, which is shorter than its diff:
```python
import functools

import jax
import jax.numpy as jnp
from jax import lax
from jax.experimental import pallas as pl
from jax.experimental.pallas import tpu as pltpu
from jax.sharding import Mesh
from jax.sharding import PartitionSpec as P


B = 256
EPSILON = 1e-05
RING = ("z", "core")
INFO = 16
PACK = 4
BASE = 32


def column_of(cell, ring, place):
    away, _, second_other, _ = cell
    core = place[1]
    distance = lax.rem((1 - 2 * core) * away + ring, ring)
    return distance * 2 + (1 - core if second_other else core)


def tile_kernel(cells, where, ring, place, residual, *refs):
    out = refs[-1]
    parts = out.shape[0]
    depth = B // parts
    count = residual.shape[1]
    entries = []
    for first in range(0, len(cells), PACK):
        packed = jnp.zeros((8, 128), jnp.float32)
        for j in range(first, min(first + PACK, len(cells))):
            start = cells[j][3]
            line = refs[where[j][2]][start : start + INFO, 0:128].astype(jnp.float32)[0:8]
            spot = lax.broadcasted_iota(jnp.int32, line.shape, 1) == column_of(cells[j], ring, place)
            packed = packed + jnp.where(spot, line * float(BASE ** (j - first)), 0.0)
        total = jnp.sum(packed).astype(jnp.int32)
        for j in range(first, min(first + PACK, len(cells))):
            entries.append(lax.rem(total // BASE ** (j - first), BASE))
    for j, (a_at, c_at, _) in enumerate(where):
        entry = entries[j]
        rows = slice(2 * j * depth, 2 * (j + 1) * depth)

        @pl.when(entry > 0)
        def _(a_ref=refs[a_at], c_ref=refs[c_at], j=j, entry=entry):
            first = pl.multiple_of((entry - 1) // 4 * B, B)
            second = pl.multiple_of(lax.rem(entry - 1, 4) * B, B)
            left = a_ref[0:count, pl.ds(first, B)].T.astype(jnp.float32)
            weighted = (residual[...] * left).astype(jnp.bfloat16)
            right = c_ref[0:count, pl.ds(second, B)]
            cross = jnp.dot(weighted, right, preferred_element_type=jnp.float32)
            spread = jnp.dot(
                weighted * weighted, right * right, preferred_element_type=jnp.float32
            )
            cross = cross.astype(jnp.bfloat16).reshape(parts, depth, B)
            spread = spread.astype(jnp.bfloat16).reshape(parts, depth, B)
            out[:, 2 * j * depth : (2 * j + 1) * depth, :] = cross
            out[:, (2 * j + 1) * depth : (2 * j + 2) * depth, :] = spread

        @pl.when(entry == 0)
        def _(rows=rows):
            out[:, rows, :] = jnp.zeros((parts, 2 * depth, B), jnp.bfloat16)


def tiles(cells, operands, ring, parts, place, residual):
    arrays, where = [], []
    for triple in operands:
        spots = []
        for x in triple:
            spot = next((i for i, y in enumerate(arrays) if y is x), len(arrays))
            if spot == len(arrays):
                arrays.append(x)
            spots.append(spot)
        where.append(tuple(spots))
    rows = residual.shape[1]
    shape = (parts, len(cells) * 2 * (B // parts), B)
    smem = pl.BlockSpec(memory_space=pltpu.SMEM)
    vmem = pl.BlockSpec(memory_space=pltpu.VMEM)
    return pl.pallas_call(
        functools.partial(tile_kernel, cells, where, ring),
        out_shape=jax.ShapeDtypeStruct(shape, jnp.bfloat16),
        in_specs=[smem, vmem] + [vmem] * len(arrays),
        out_specs=vmem,
        cost_estimate=pl.CostEstimate(
            flops=len(cells) * 4 * rows * B * B,
            bytes_accessed=len(cells) * (2 * rows * B * 2 + 2 * B * B * 2),
            transcendentals=0,
        ),
        compiler_params=pltpu.CompilerParams(vmem_limit_bytes=10 << 20),
    )(place, residual, *arrays)


def scores_of(dosage, residual, pairs, counts):
    ring = lax.axis_size("z")
    parts = lax.axis_size("ind")
    chip, core = lax.axis_index("z"), lax.axis_index("core")
    total_rows = dosage.shape[0] * parts
    local_blocks = dosage.shape[1] // B
    slot_count = pairs.shape[0]
    depth = B // parts

    def move(x, by, cross=False):
        perm = []
        for z in range(ring):
            for k in range(2):
                to = (z + (by if k == 0 else -by)) % ring
                perm.append((z * 2 + k, to * 2 + (1 - k if cross else k)))
        return lax.ppermute(x, RING, perm)

    def swap(x):
        return move(x, 0, True)

    live = jnp.arange(slot_count, dtype=jnp.int32) < counts[0]
    first_local = pairs[:, 0] - (chip * 2 + core) * local_blocks
    second_local = pairs[:, 1] % local_blocks
    holder = pairs[:, 1] // local_blocks
    away = (holder // 2 - chip) % ring
    position = away * 2 + holder % 2
    wanted = (position[:, None] == jnp.arange(2 * ring, dtype=jnp.int32)[None, :]) & live[:, None]
    code = 1 + first_local * local_blocks + second_local
    row = jnp.sum(jnp.where(wanted, code[:, None], 0), axis=0)
    info = jnp.pad(row.astype(jnp.bfloat16)[None, :], ((0, INFO - 1), (0, dosage.shape[1] - 2 * ring)))
    place = jnp.stack([chip, core]).astype(jnp.int32)
    weights = residual[None, :]

    hops = ring // 4
    across = swap(jnp.concatenate([dosage, info]))
    own, other = [dosage], [jnp.concatenate([across, info])]
    ahead_info = move(info, 1)
    far_own, far_other = [dosage], [other[0]]
    count = dosage.shape[0]
    results = {}

    def exchange(cells, operands):
        partial = tiles(tuple(cells), operands, ring, parts, place, weights)
        arrived = lax.all_to_all(partial, "ind", 0, 0, tiled=True)
        summed = jnp.sum(arrived.astype(jnp.float32), axis=0)
        summed = summed.reshape(len(cells), 2, depth, B)
        scores = summed[:, 0] / jnp.sqrt(summed[:, 1] + EPSILON * total_rows)
        scores = scores.astype(jnp.bfloat16)
        for j in range(0, len(cells), 2):
            results[cells[j][:2]] = scores[j : j + 2]

    def both(away_by, first_other, a, at, table, start):
        for second_other in (False, True):
            c = far_other[at] if second_other else far_own[at]
            cells.append((away_by, first_other, second_other, start))
            operands.append((a, c, table))

    near, cross = {}, {}
    for h in range(1, hops + 1):
        own.append(move(own[h - 1], 1))
        other.append(move(other[h - 1], 1))
        cells, operands = [], []
        if h == 1:
            both(0, False, dosage, 0, other[0], count + INFO)
            both(1, False, own[1], 0, ahead_info, 0)
            exchange(cells, operands)
            near[0] = results[0, False]
            cells, operands = [], []
        far_other.append(swap(own[h]))
        far_own.append(swap(other[h]))
        for first_other in (False, True):
            a = other[h] if first_other else own[h]
            start = count + (0 if first_other else INFO)
            if h > 1 or first_other:
                both(2 * h - 1, first_other, a, h - 1, other[h], start)
            if h < hops or not first_other:
                both(2 * h, first_other, a, h, other[h], start)
        exchange(cells, operands)
        odd, even = 2 * h - 1, 2 * h
        sent = [results[odd, False], results[even, False]]
        if h < hops:
            sent.append(results[even, True])
        sent.append(results[odd, True])
        came = move(jnp.concatenate(sent), -h)
        near[h], cross[h] = came[:4], came[4:]
    crossed = swap(jnp.concatenate([cross[h] for h in range(hops, 0, -1)]))
    found = jnp.concatenate([near[h] for h in range(hops + 1)] + [crossed], axis=0)
    ahead = jnp.where(core == 0, away, -away) % ring
    unlike = (holder % 2 != core).astype(jnp.int32)
    index = ahead * 2 + jnp.where(ahead <= 2 * hops, unlike, 1 - unlike)
    picked = jnp.take(found, index, axis=0)
    picked = jnp.where(live[:, None, None], picked, jnp.bfloat16(0.0))
    return jnp.transpose(picked, (1, 0, 2))


def solution(mesh):
    devices = mesh.devices.reshape(mesh.shape["ind"], mesh.shape["blk"] // 2, 2)
    torus = Mesh(devices, ("ind", *RING))
    placed = (P("ind", RING), P("ind"), P(RING, None), P(RING))
    return jax.shard_map(scores_of, mesh=torus, in_specs=placed, out_specs=P("ind", RING, None), check_vma=False)
```

time: 230 us -> 225 us (0.978); the launches traced: 227 us -> 224 us
  waiting for transfers between devices: 61.7 us -> 85.3 us
  starting transfers between devices: 120 us -> 104 us
  local copies, waits for them, and re-layouts: 12.1 us -> 5.49 us
    ppermute x25 -> x23, starting transfers between devices: 94.3 us -> 77.5 us  [move(): return lax.ppermute(x, RING, perm)]
    all_to_all x5, waiting for transfers between devices: 32.4 us -> 46 us  [exchange(): arrived = lax.all_to_all(partial, 'ind', 0, 0, tiled=True)]
    ppermute x25 -> x23, waiting for transfers between devices: 29.3 us -> 39.4 us  [move(): return lax.ppermute(x, RING, perm)]
    unnamed x30 -> x18, local copies, waits for them, and re-layouts: 9.34 us -> 4.17 us
  transfers between devices with their start and end apart: 30 -> 28, of which waited for: 10 -> 12; matrix products, arithmetic and copies ran while one was open for 4% -> 3% of each run, Pallas kernels for 8% -> 8%
where the time goes in v4:
time: 225 us; the launch traced here: 224 us
  starting transfers between devices  104 us (46%)
  waiting for transfers between devices  85.3 us (38%)
  Pallas kernels  17.5 us (8%)
  other arithmetic  10.4 us (5%)
  local copies, waits for them, and re-layouts  5.49 us (2%)
    ppermute x23, starting transfers between devices, move(): return lax.ppermute(x, RING, perm)  77.5 us
    all_to_all x5, waiting for transfers between devices, exchange(): arrived = lax.all_to_all(partial, 'ind', 0, 0, tiled=True)  46 us
    ppermute x23, waiting for transfers between devices, move(): return lax.ppermute(x, RING, perm)  39.4 us
    all_to_all x5, starting transfers between devices, exchange(): arrived = lax.all_to_all(partial, 'ind', 0, 0, tiled=True)  26.5 us
    pallas_call x5, Pallas kernels, tiles(): pl.pallas_call(functools.partial(tile_kernel, cells, where, ring), out_sh...  17.5 us
    reduce_sum x5, other arithmetic, exchange(): summed = jnp.sum(arrived.astype(jnp.float32), axis=0)  7.03 us
  transfers between devices with their start and end apart: 28, of which 12 were waited for; matrix products, arithmetic and copies ran while one was open for 3% of the time, Pallas kernels for 8%

profile of v4, /device:TPU:1, one launch (start us, length us, event | category | flops | bytes accessed | tf_op | source)
XLA Modules:
  0.0 224.0 jit_solution(3126981066386161601)
XLA Ops:
  3.6 8.9 %collective-permute-start = (bf16[528,1024]{1,0:T(8,128)(2,1)S(1)}, bf16[528,1024]{1,0:T(8,128)(2,1)S(1)}, u32[]{:S(2)}, u32[]{:S(2)}) collective-permute-start(bf16[528,1024]{1,0:T(8,128)(2,1)S(1)} %pad_maximum_fusion.1), channel_id=1, source_target_pairs={{0,1},{1,0},{2,3},{3,2},{4,5},{5,4},{6,7},{7,6},{8,9},{9,8},{10,11... | collective-permute-start | bytes 3244040 | tf_op jit(solution)/shard_map/ppermute | solution.py:111
  14.9 5.8 %collective-permute-start.3 = (bf16[544,1024]{1,0:T(8,128)(2,1)S(1)}, bf16[544,1024]{1,0:T(8,128)(2,1)}, u32[]{:S(2)}, u32[]{:S(2)}) collective-permute-start(bf16[544,1024]{1,0:T(8,128)(2,1)S(1)} %pad_maximum_fusion.refs_1_.refs_5_), channel_id=1, source_target_pairs={{0,2},{1,31},{2,4},{3,1},{4,6},{5,3},{6,8},{7,5},{8,10},{9,7},{10,... | collective-permute-start | bytes 3342344 | tf_op jit(solution)/shard_map/ppermute | solution.py:111
  23.3 9.8 %collective-permute-done.3.refs_2_ = bf16[544,1024]{1,0:T(8,128)(2,1)} collective-permute-done((bf16[544,1024]{1,0:T(8,128)(2,1)S(1)}, bf16[544,1024]{1,0:T(8,128)(2,1)}, u32[]{:S(2)}, u32[]{:S(2)}) %collective-permute-start.3) | collective-permute-done | bytes 1114144 | tf_op jit(solution)/shard_map/ppermute | solution.py:111
  33.1 3.7 %collective-permute-start.4 = (bf16[544,1024]{1,0:T(8,128)(2,1)}, bf16[544,1024]{1,0:T(8,128)(2,1)S(1)}, u32[]{:S(2)}, u32[]{:S(2)}) collective-permute-start(bf16[544,1024]{1,0:T(8,128)(2,1)} %collective-permute-done.3.refs_2_), channel_id=1, source_target_pairs={{0,1},{1,0},{2,3},{3,2},{4,5},{5,4},{6,7},{7,6},{8,9},{9,8},{10,11... | collective-permute-start | bytes 3342344 | tf_op jit(solution)/shard_map/ppermute | solution.py:111
  40.4 3.9 %collective-permute-done.1.refs_2_.refs_0_ = bf16[512,1024]{1,0:T(8,128)(2,1)} collective-permute-done((bf16[512,1024]{1,0:T(8,128)(2,1)S(1)}, bf16[512,1024]{1,0:T(8,128)(2,1)}, u32[]{:S(2)}, u32[]{:S(2)}) %collective-permute-start.1) | collective-permute-done | bytes 1048608 | tf_op jit(solution)/shard_map/ppermute | solution.py:111
  44.3 3.7 %collective-permute-start.5 = (bf16[512,1024]{1,0:T(8,128)(2,1)}, bf16[512,1024]{1,0:T(8,128)(2,1)}, u32[]{:S(2)}, u32[]{:S(2)}) collective-permute-start(bf16[512,1024]{1,0:T(8,128)(2,1)} %collective-permute-done.1.refs_2_.refs_0_), channel_id=1, source_target_pairs={{0,1},{1,0},{2,3},{3,2},{4,5},{5,4},{6,7},{7,6},{8,9},{9,8},{10,11... | collective-permute-start | bytes 3145736 | tf_op jit(solution)/shard_map/ppermute | solution.py:111
  50.9 6.8 %all-to-all-start = ((bf16[16,128,256]{2,1,0:T(8,128)(2,1)}), bf16[16,128,256]{2,1,0:T(8,128)(2,1)}, u32[]{:S(2)}, u32[]{:S(2)}) async-start(bf16[16,128,256]{2,1,0:T(8,128)(2,1)} %copy-done.6), calls=%async_computation | async-start | bytes 2097152 | tf_op jit(solution)/shard_map/all_to_all | solution.py:139
  69.1 5.1 %all-to-all-done = bf16[16,128,256]{2,1,0:T(8,128)(2,1)} async-done(((bf16[16,128,256]{2,1,0:T(8,128)(2,1)}), bf16[16,128,256]{2,1,0:T(8,128)(2,1)}, u32[]{:S(2)}, u32[]{:S(2)}) %all-to-all-start) | async-done | bytes 1048608 | tf_op jit(solution)/shard_map/all_to_all | solution.py:139
  74.2 4.5 %all-to-all-start.1 = ((bf16[16,192,256]{2,1,0:T(8,128)(2,1)}), bf16[16,192,256]{2,1,0:T(8,128)(2,1)}, u32[]{:S(2)}, u32[]{:S(2)}) async-start(bf16[16,192,256]{2,1,0:T(8,128)(2,1)} %copy-done.1), calls=%async_computation.1 | async-start | bytes 3145728 | tf_op jit(solution)/shard_map/all_to_all | solution.py:139
  78.7 3.8 %collective-permute-start.9 = (bf16[544,1024]{1,0:T(8,128)(2,1)}, bf16[544,1024]{1,0:T(8,128)(2,1)S(1)}, u32[]{:S(2)}, u32[]{:S(2)}) collective-permute-start(bf16[544,1024]{1,0:T(8,128)(2,1)} %collective-permute-done.8.refs_2_), channel_id=1, source_target_pairs={{0,1},{1,0},{2,3},{3,2},{4,5},{5,4},{6,7},{7,6},{8,9},{9,8},{10,11... | collective-permute-start | bytes 3342344 | tf_op jit(solution)/shard_map/ppermute | solution.py:111
  85.8 4.6 %collective-permute-start.10 = (bf16[512,1024]{1,0:T(8,128)(2,1)}, bf16[512,1024]{1,0:T(8,128)(2,1)S(1)}, u32[]{:S(2)}, u32[]{:S(2)}) collective-permute-start(bf16[512,1024]{1,0:T(8,128)(2,1)} %collective-permute-done.7.refs_0_), channel_id=1, source_target_pairs={{0,1},{1,0},{2,3},{3,2},{4,5},{5,4},{6,7},{7,6},{8,9},{9,8},{10,11... | collective-permute-start | bytes 3145736 | tf_op jit(solution)/shard_map/ppermute | solution.py:111
  95.3 4.9 %shard_map.48 = bf16[16,256,256]{2,1,0:T(8,128)(2,1)} custom-call(s32[2]{0:T(128)S(1)} %pad_add_fusion.place, f32[1,512]{1,0:T(1,128)S(1)} %bitcast.123, bf16[512,1024]{1,0:T(8,128)(2,1)} %collective-permute-done.7.refs_0_, bf16[544,1024]{1,0:T(8,128)(2,1)S(1)} %collective-permute-done.4.refs_1_, bf16[544,1024]{1,0:T(8,128)(2,1)} %collective-permute-done.8.refs_2_, ...), custom_call_target="tpu_custom_call" | custom-call | flops 1073741824 | bytes 6291456 | tf_op jit(solution)/shard_map/pallas_call | solution.py:82
  102.1 7.0 %all-to-all-start.2 = ((bf16[16,256,256]{2,1,0:T(8,128)(2,1)}), bf16[16,256,256]{2,1,0:T(8,128)(2,1)}, u32[]{:S(2)}, u32[]{:S(2)}) async-start(bf16[16,256,256]{2,1,0:T(8,128)(2,1)} %shard_map.48), calls=%async_computation.2 | async-start | bytes 4194304 | tf_op jit(solution)/shard_map/all_to_all | solution.py:139
  111.3 7.2 %collective-permute-done.12.refs_0_ = bf16[512,1024]{1,0:T(8,128)(2,1)} collective-permute-done((bf16[512,1024]{1,0:T(8,128)(2,1)}, bf16[512,1024]{1,0:T(8,128)(2,1)}, u32[]{:S(2)}, u32[]{:S(2)}) %collective-permute-start.12) | collective-permute-done | bytes 1048608 | tf_op jit(solution)/shard_map/ppermute | solution.py:111
  118.5 4.0 %collective-permute-start.15 = (bf16[512,1024]{1,0:T(8,128)(2,1)}, bf16[512,1024]{1,0:T(8,128)(2,1)S(1)}, u32[]{:S(2)}, u32[]{:S(2)}) collective-permute-start(bf16[512,1024]{1,0:T(8,128)(2,1)} %collective-permute-done.12.refs_0_), channel_id=1, source_target_pairs={{0,1},{1,0},{2,3},{3,2},{4,5},{5,4},{6,7},{7,6},{8,9},{9,8},{10,11... | collective-permute-start | bytes 3145736 | tf_op jit(solution)/shard_map/ppermute | solution.py:111
  128.0 4.0 %shard_map.49 = bf16[16,256,256]{2,1,0:T(8,128)(2,1)} custom-call(s32[2]{0:T(128)S(1)} %pad_add_fusion.place, f32[1,512]{1,0:T(1,128)S(1)} %bitcast.124, bf16[512,1024]{1,0:T(8,128)(2,1)} %collective-permute-done.12.refs_0_, bf16[544,1024]{1,0:T(8,128)(2,1)S(1)} %copy-done.3, bf16[544,1024]{1,0:T(8,128)(2,1)} %collective-permute-done.13.refs_2_, ...), custom_call_target="tpu_custom_call" | custom-call | flops 1073741824 | bytes 6291456 | tf_op jit(solution)/shard_map/pallas_call | solution.py:82
  131.9 11.3 %all-to-all-done.2 = bf16[16,256,256]{2,1,0:T(8,128)(2,1)} async-done(((bf16[16,256,256]{2,1,0:T(8,128)(2,1)}), bf16[16,256,256]{2,1,0:T(8,128)(2,1)}, u32[]{:S(2)}, u32[]{:S(2)}) %all-to-all-start.2) | async-done | bytes 2097184 | tf_op jit(solution)/shard_map/all_to_all | solution.py:139
  143.2 4.4 %all-to-all-start.3 = ((bf16[16,256,256]{2,1,0:T(8,128)(2,1)}), bf16[16,256,256]{2,1,0:T(8,128)(2,1)}, u32[]{:S(2)}, u32[]{:S(2)}) async-start(bf16[16,256,256]{2,1,0:T(8,128)(2,1)} %shard_map.49), calls=%async_computation.3 | async-start | bytes 4194304 | tf_op jit(solution)/shard_map/all_to_all | solution.py:139
  162.1 18.5 %all-to-all-done.3 = bf16[16,256,256]{2,1,0:T(8,128)(2,1)} async-done(((bf16[16,256,256]{2,1,0:T(8,128)(2,1)}), bf16[16,256,256]{2,1,0:T(8,128)(2,1)}, u32[]{:S(2)}, u32[]{:S(2)}) %all-to-all-start.3) | async-done | bytes 2097184 | tf_op jit(solution)/shard_map/all_to_all | solution.py:139
  180.6 3.7 %all-to-all-start.4 = ((bf16[16,192,256]{2,1,0:T(8,128)(2,1)}), bf16[16,192,256]{2,1,0:T(8,128)(2,1)S(1)}, u32[]{:S(2)}, u32[]{:S(2)}) async-start(bf16[16,192,256]{2,1,0:T(8,128)(2,1)} %shard_map.50), calls=%async_computation.4 | async-start | bytes 3145728 | tf_op jit(solution)/shard_map/all_to_all | solution.py:139
  186.3 5.2 %collective-permute-done.11 = bf16[8,16,256]{2,1,0:T(8,128)(2,1)S(1)} collective-permute-done((bf16[8,16,256]{2,1,0:T(8,128)(2,1)S(1)}, bf16[8,16,256]{2,1,0:T(8,128)(2,1)S(1)}, u32[]{:S(2)}, u32[]{:S(2)}) %collective-permute-start.11) | collective-permute-done | bytes 65568 | tf_op jit(solution)/shard_map/ppermute | solution.py:111
  195.4 11.1 %all-to-all-done.4 = bf16[16,192,256]{2,1,0:T(8,128)(2,1)S(1)} async-done(((bf16[16,192,256]{2,1,0:T(8,128)(2,1)}), bf16[16,192,256]{2,1,0:T(8,128)(2,1)S(1)}, u32[]{:S(2)}, u32[]{:S(2)}) %all-to-all-start.4) | async-done | bytes 1572896 | tf_op jit(solution)/shard_map/all_to_all | solution.py:139
  208.6 6.8 %collective-permute-done.21 = bf16[6,16,256]{2,1,0:T(8,128)(2,1)S(1)} collective-permute-done((bf16[6,16,256]{2,1,0:T(8,128)(2,1)S(1)}, bf16[6,16,256]{2,1,0:T(8,128)(2,1)S(1)}, u32[]{:S(2)}, u32[]{:S(2)}) %collective-permute-start.21) | collective-permute-done | bytes 49184 | tf_op jit(solution)/shard_map/ppermute | solution.py:111
  215.5 6.2 %collective-permute-start.22 = (bf16[14,16,256]{2,1,0:T(8,128)(2,1)S(1)}, bf16[14,16,256]{2,1,0:T(8,128)(2,1)S(1)}, u32[]{:S(2)}, u32[]{:S(2)}) collective-permute-start(bf16[14,16,256]{2,1,0:T(8,128)(2,1)S(1)} %pad_maximum_fusion.2), channel_id=1, source_target_pairs={{0,1},{1,0},{2,3},{3,2},{4,5},{5,4},{6,7},{7,6},{8,9},{9,8},{10,11... | collective-permute-start | bytes 344072 | tf_op jit(solution)/shard_map/ppermute | solution.py:111
  (93 shorter events, 68.0 us)
Async XLA Ops:
  3.6 11.2 %collective-permute-start = (bf16[528,1024]{1,0:T(8,128)(2,1)S(1)}, bf16[528,1024]{1,0:T(8,128)(2,1)S(1)}, u32[]{:S(2)}, u32[]{:S(2)}) collective-permute-start(bf16[528,1024]{1,0:T(8,128)(2,1)S(1)} %pad_maximum_fusion.1), channel_id=1, source_target_pairs={{0,1},{1,0},{2,3},{3,2},{4,5},{5,4},{6,7},{7,6},{8,9},{9,8},{10,11... | collective-permute-start | bytes 3244040 | tf_op jit(solution)/shard_map/ppermute | solution.py:111
  14.9 18.2 %collective-permute-start.3 = (bf16[544,1024]{1,0:T(8,128)(2,1)S(1)}, bf16[544,1024]{1,0:T(8,128)(2,1)}, u32[]{:S(2)}, u32[]{:S(2)}) collective-permute-start(bf16[544,1024]{1,0:T(8,128)(2,1)S(1)} %pad_maximum_fusion.refs_1_.refs_5_), channel_id=1, source_target_pairs={{0,2},{1,31},{2,4},{3,1},{4,6},{5,3},{6,8},{7,5},{8,10},{9,7},{10,... | collective-permute-start | bytes 3342344 | tf_op jit(solution)/shard_map/ppermute | solution.py:111
  20.7 23.6 %collective-permute-start.1 = (bf16[512,1024]{1,0:T(8,128)(2,1)S(1)}, bf16[512,1024]{1,0:T(8,128)(2,1)}, u32[]{:S(2)}, u32[]{:S(2)}) collective-permute-start(bf16[512,1024]{1,0:T(8,128)(2,1)S(1)} %copy-done), channel_id=1, source_target_pairs={{0,2},{1,31},{2,4},{3,1},{4,6},{5,3},{6,8},{7,5},{8,10},{9,7},{10,... | collective-permute-start | bytes 3145736 | tf_op jit(solution)/shard_map/ppermute | solution.py:111
  33.1 31.3 %collective-permute-start.4 = (bf16[544,1024]{1,0:T(8,128)(2,1)}, bf16[544,1024]{1,0:T(8,128)(2,1)S(1)}, u32[]{:S(2)}, u32[]{:S(2)}) collective-permute-start(bf16[544,1024]{1,0:T(8,128)(2,1)} %collective-permute-done.3.refs_2_), channel_id=1, source_target_pairs={{0,1},{1,0},{2,3},{3,2},{4,5},{5,4},{6,7},{7,6},{8,9},{9,8},{10,11... | collective-permute-start | bytes 3342344 | tf_op jit(solution)/shard_map/ppermute | solution.py:111
  36.8 11.3 %collective-permute-start.2 = (bf16[16,1024]{1,0:T(8,128)(2,1)S(1)}, bf16[16,1024]{1,0:T(8,128)(2,1)S(1)}, u32[]{:S(2)}, u32[]{:S(2)}) collective-permute-start(bf16[16,1024]{1,0:T(8,128)(2,1)S(1)} %pad.4), channel_id=1, source_target_pairs={{0,2},{1,31},{2,4},{3,1},{4,6},{5,3},{6,8},{7,5},{8,10},{9,7},{10,... | collective-permute-start | bytes 98312 | tf_op jit(solution)/shard_map/ppermute | solution.py:111
  44.3 20.0 %collective-permute-start.5 = (bf16[512,1024]{1,0:T(8,128)(2,1)}, bf16[512,1024]{1,0:T(8,128)(2,1)}, u32[]{:S(2)}, u32[]{:S(2)}) collective-permute-start(bf16[512,1024]{1,0:T(8,128)(2,1)} %collective-permute-done.1.refs_2_.refs_0_), channel_id=1, source_target_pairs={{0,1},{1,0},{2,3},{3,2},{4,5},{5,4},{6,7},{7,6},{8,9},{9,8},{10,11... | collective-permute-start | bytes 3145736 | tf_op jit(solution)/shard_map/ppermute | solution.py:111
  50.9 23.2 %all-to-all-start = ((bf16[16,128,256]{2,1,0:T(8,128)(2,1)}), bf16[16,128,256]{2,1,0:T(8,128)(2,1)}, u32[]{:S(2)}, u32[]{:S(2)}) async-start(bf16[16,128,256]{2,1,0:T(8,128)(2,1)} %copy-done.6), calls=%async_computation | async-start | bytes 2097152 | tf_op jit(solution)/shard_map/all_to_all | solution.py:139
  57.7 21.0 %collective-permute-start.8 = (bf16[544,1024]{1,0:T(8,128)(2,1)}, bf16[544,1024]{1,0:T(8,128)(2,1)}, u32[]{:S(2)}, u32[]{:S(2)}) collective-permute-start(bf16[544,1024]{1,0:T(8,128)(2,1)} %collective-permute-done.3.refs_2_), channel_id=1, source_target_pairs={{0,2},{1,31},{2,4},{3,1},{4,6},{5,3},{6,8},{7,5},{8,10},{9,7},{10,... | collective-permute-start | bytes 3342344 | tf_op jit(solution)/shard_map/ppermute | solution.py:111
  61.4 24.4 %collective-permute-start.7 = (bf16[512,1024]{1,0:T(8,128)(2,1)}, bf16[512,1024]{1,0:T(8,128)(2,1)}, u32[]{:S(2)}, u32[]{:S(2)}) collective-permute-start(bf16[512,1024]{1,0:T(8,128)(2,1)} %collective-permute-done.1.refs_2_.refs_0_), channel_id=1, source_target_pairs={{0,2},{1,31},{2,4},{3,1},{4,6},{5,3},{6,8},{7,5},{8,10},{9,7},{10,... | collective-permute-start | bytes 3145736 | tf_op jit(solution)/shard_map/ppermute | solution.py:111
  74.2 28.0 %all-to-all-start.1 = ((bf16[16,192,256]{2,1,0:T(8,128)(2,1)}), bf16[16,192,256]{2,1,0:T(8,128)(2,1)}, u32[]{:S(2)}, u32[]{:S(2)}) async-start(bf16[16,192,256]{2,1,0:T(8,128)(2,1)} %copy-done.1), calls=%async_computation.1 | async-start | bytes 3145728 | tf_op jit(solution)/shard_map/all_to_all | solution.py:139
  78.7 16.6 %collective-permute-start.9 = (bf16[544,1024]{1,0:T(8,128)(2,1)}, bf16[544,1024]{1,0:T(8,128)(2,1)S(1)}, u32[]{:S(2)}, u32[]{:S(2)}) collective-permute-start(bf16[544,1024]{1,0:T(8,128)(2,1)} %collective-permute-done.8.refs_2_), channel_id=1, source_target_pairs={{0,1},{1,0},{2,3},{3,2},{4,5},{5,4},{6,7},{7,6},{8,9},{9,8},{10,11... | collective-permute-start | bytes 3342344 | tf_op jit(solution)/shard_map/ppermute | solution.py:111
  85.8 9.5 %collective-permute-start.10 = (bf16[512,1024]{1,0:T(8,128)(2,1)}, bf16[512,1024]{1,0:T(8,128)(2,1)S(1)}, u32[]{:S(2)}, u32[]{:S(2)}) collective-permute-start(bf16[512,1024]{1,0:T(8,128)(2,1)} %collective-permute-done.7.refs_0_), channel_id=1, source_target_pairs={{0,1},{1,0},{2,3},{3,2},{4,5},{5,4},{6,7},{7,6},{8,9},{9,8},{10,11... | collective-permute-start | bytes 3145736 | tf_op jit(solution)/shard_map/ppermute | solution.py:111
  90.4 18.8 %collective-permute-start.13 = (bf16[544,1024]{1,0:T(8,128)(2,1)}, bf16[544,1024]{1,0:T(8,128)(2,1)}, u32[]{:S(2)}, u32[]{:S(2)}) collective-permute-start(bf16[544,1024]{1,0:T(8,128)(2,1)} %collective-permute-done.8.refs_2_), channel_id=1, source_target_pairs={{0,2},{1,31},{2,4},{3,1},{4,6},{5,3},{6,8},{7,5},{8,10},{9,7},{10,... | collective-permute-start | bytes 3342344 | tf_op jit(solution)/shard_map/ppermute | solution.py:111
  93.4 25.1 %collective-permute-start.12 = (bf16[512,1024]{1,0:T(8,128)(2,1)}, bf16[512,1024]{1,0:T(8,128)(2,1)}, u32[]{:S(2)}, u32[]{:S(2)}) collective-permute-start(bf16[512,1024]{1,0:T(8,128)(2,1)} %collective-permute-done.7.refs_0_), channel_id=1, source_target_pairs={{0,2},{1,31},{2,4},{3,1},{4,6},{5,3},{6,8},{7,5},{8,10},{9,7},{10,... | collective-permute-start | bytes 3145736 | tf_op jit(solution)/shard_map/ppermute | solution.py:111
  102.1 41.0 %all-to-all-start.2 = ((bf16[16,256,256]{2,1,0:T(8,128)(2,1)}), bf16[16,256,256]{2,1,0:T(8,128)(2,1)}, u32[]{:S(2)}, u32[]{:S(2)}) async-start(bf16[16,256,256]{2,1,0:T(8,128)(2,1)} %shard_map.48), calls=%async_computation.2 | async-start | bytes 4194304 | tf_op jit(solution)/shard_map/all_to_all | solution.py:139
  109.2 18.7 %collective-permute-start.14 = (bf16[544,1024]{1,0:T(8,128)(2,1)}, bf16[544,1024]{1,0:T(8,128)(2,1)S(1)}, u32[]{:S(2)}, u32[]{:S(2)}) collective-permute-start(bf16[544,1024]{1,0:T(8,128)(2,1)} %collective-permute-done.13.refs_2_), channel_id=1, source_target_pairs={{0,1},{1,0},{2,3},{3,2},{4,5},{5,4},{6,7},{7,6},{8,9},{9,8},{10,11... | collective-permute-start | bytes 3342344 | tf_op jit(solution)/shard_map/ppermute | solution.py:111
  118.5 9.4 %collective-permute-start.15 = (bf16[512,1024]{1,0:T(8,128)(2,1)}, bf16[512,1024]{1,0:T(8,128)(2,1)S(1)}, u32[]{:S(2)}, u32[]{:S(2)}) collective-permute-start(bf16[512,1024]{1,0:T(8,128)(2,1)} %collective-permute-done.12.refs_0_), channel_id=1, source_target_pairs={{0,1},{1,0},{2,3},{3,2},{4,5},{5,4},{6,7},{7,6},{8,9},{9,8},{10,11... | collective-permute-start | bytes 3145736 | tf_op jit(solution)/shard_map/ppermute | solution.py:111
  122.5 25.2 %collective-permute-start.17 = (bf16[512,1024]{1,0:T(8,128)(2,1)}, bf16[512,1024]{1,0:T(8,128)(2,1)}, u32[]{:S(2)}, u32[]{:S(2)}) collective-permute-start(bf16[512,1024]{1,0:T(8,128)(2,1)} %collective-permute-done.12.refs_0_), channel_id=1, source_target_pairs={{0,2},{1,31},{2,4},{3,1},{4,6},{5,3},{6,8},{7,5},{8,10},{9,7},{10,... | collective-permute-start | bytes 3145736 | tf_op jit(solution)/shard_map/ppermute | solution.py:111
  126.0 25.7 %collective-permute-start.18 = (bf16[544,1024]{1,0:T(8,128)(2,1)}, bf16[544,1024]{1,0:T(8,128)(2,1)}, u32[]{:S(2)}, u32[]{:S(2)}) collective-permute-start(bf16[544,1024]{1,0:T(8,128)(2,1)} %collective-permute-done.13.refs_2_), channel_id=1, source_target_pairs={{0,2},{1,31},{2,4},{3,1},{4,6},{5,3},{6,8},{7,5},{8,10},{9,7},{10,... | collective-permute-start | bytes 3342344 | tf_op jit(solution)/shard_map/ppermute | solution.py:111
  143.2 37.4 %all-to-all-start.3 = ((bf16[16,256,256]{2,1,0:T(8,128)(2,1)}), bf16[16,256,256]{2,1,0:T(8,128)(2,1)}, u32[]{:S(2)}, u32[]{:S(2)}) async-start(bf16[16,256,256]{2,1,0:T(8,128)(2,1)} %shard_map.49), calls=%async_computation.3 | async-start | bytes 4194304 | tf_op jit(solution)/shard_map/all_to_all | solution.py:139
  147.7 11.0 %collective-permute-start.20 = (bf16[512,1024]{1,0:T(8,128)(2,1)}, bf16[512,1024]{1,0:T(8,128)(2,1)S(1)}, u32[]{:S(2)}, u32[]{:S(2)}) collective-permute-start(bf16[512,1024]{1,0:T(8,128)(2,1)} %collective-permute-done.17.refs_0_), channel_id=1, source_target_pairs={{0,1},{1,0},{2,3},{3,2},{4,5},{5,4},{6,7},{7,6},{8,9},{9,8},{10,11... | collective-permute-start | bytes 3145736 | tf_op jit(solution)/shard_map/ppermute | solution.py:111
  154.6 31.7 %collective-permute-start.6 = (bf16[8,16,256]{2,1,0:T(8,128)(2,1)S(1)}, bf16[8,16,256]{2,1,0:T(8,128)(2,1)S(1)}, u32[]{:S(2)}, u32[]{:S(2)}) collective-permute-start(bf16[8,16,256]{2,1,0:T(8,128)(2,1)S(1)} %pad_maximum_fusion.3), channel_id=1, source_target_pairs={{0,30},{1,3},{2,0},{3,5},{4,2},{5,7},{6,4},{7,9},{8,6},{9,11},{10,... | collective-permute-start | bytes 196616 | tf_op jit(solution)/shard_map/ppermute | solution.py:111
  180.6 25.8 %all-to-all-start.4 = ((bf16[16,192,256]{2,1,0:T(8,128)(2,1)}), bf16[16,192,256]{2,1,0:T(8,128)(2,1)S(1)}, u32[]{:S(2)}, u32[]{:S(2)}) async-start(bf16[16,192,256]{2,1,0:T(8,128)(2,1)} %shard_map.50), calls=%async_computation.4 | async-start | bytes 3145728 | tf_op jit(solution)/shard_map/all_to_all | solution.py:139
  193.4 15.2 %collective-permute-start.16 = (bf16[8,16,256]{2,1,0:T(8,128)(2,1)S(1)}, bf16[8,16,256]{2,1,0:T(8,128)(2,1)S(1)}, u32[]{:S(2)}, u32[]{:S(2)}) collective-permute-start(bf16[8,16,256]{2,1,0:T(8,128)(2,1)S(1)} %pad_maximum_fusion.5), channel_id=1, source_target_pairs={{0,26},{1,7},{2,28},{3,9},{4,30},{5,11},{6,0},{7,13},{8,2},{9,15},... | collective-permute-start | bytes 196616 | tf_op jit(solution)/shard_map/ppermute | solution.py:111
  (12 other events, 140.4 us)
